TPU v7x, 32 devices: a whole 2x2x4 slice. The times are simulated.
32 devices in a mesh: stream: 2 (over y), dp: 8 (over z, x), head: 2 (over core).
Axes of the slice: x: 2, y: 2, z: 4, core: 2. Of those that a mesh axis runs over, the one named last changes fastest.
Arguments:
- patches: bfloat16 [32, 512, 768], P(('dp', 'head')), may hold values from -6 to 6
- order: int32 [32, 512], P(('dp', 'head')), may hold values from 0 to 511, each once within a row
- cotangent: bfloat16 [2, 32, 256, 768], P('stream', ('dp', 'head')), may hold values from -6 to 6
- norm_gains: float32 [2, 2, 768], P('stream'), may hold values from 0.5 to 1.5
- norm_biases: float32 [2, 2, 768], P('stream'), may hold values from -3 to 3
- layer_scales: float32 [2, 2, 768], P('stream'), may hold values from 0.5 to 1.5
- qkv_weight: bfloat16 [2, 3, 768, 768], P('stream', None, None, 'head'), may hold values from -0.21875 to 0.21875
- out_weight: bfloat16 [2, 768, 768], P('stream', 'head'), may hold values from -2.5 to 2.5
- up_weight: bfloat16 [2, 768, 3072], P('stream', None, 'head'), may hold values from -0.21875 to 0.21875
- up_bias: bfloat16 [2, 3072], P('stream', 'head'), may hold values from -3 to 3
- down_weight: bfloat16 [2, 3072, 768], P('stream', 'head'), may hold values from -0.109375 to 0.109375
- down_bias: float32 [2, 768], P('stream'), may hold values from -2 to 2
- mask_token: float32 [768], replicated, may hold values from -6 to 6
Outputs:
- latents: bfloat16 [32, 256, 768], P(('dp', 'head'))
- features: bfloat16 [2, 32, 256, 768], P('stream', ('dp', 'head'))
- input_grads: float32 [2, 32, 512, 768], P('stream', ('dp', 'head'))
- norm_gains_grad: float32 [2, 2, 768], P('stream')
- norm_biases_grad: float32 [2, 2, 768], P('stream')
- layer_scales_grad: float32 [2, 2, 768], P('stream')
- qkv_grad: float32 [2, 3, 768, 768], P('stream', None, None, 'head')
- out_grad: float32 [2, 768, 768], P('stream', 'head')
- up_grad: float32 [2, 768, 3072], P('stream', None, 'head')
- up_bias_grad: float32 [2, 3072], P('stream', 'head')
- down_grad: float32 [2, 3072, 768], P('stream', 'head')
- down_bias_grad: float32 [2, 768], P('stream')
- mask_token_grad: float32 [768], replicated
Inputs may be any that keep to these rules, and one draw needn't show every extreme that they name: `order`: each row holds every patch position of its image once; the first half of a row are the visible patches, the second half the masked ones.
All inputs are finite; a program needn't handle non-finite values.
Results may differ from a plain program's by a relative error of at most 0.014.
Values may be sent and summed in bfloat16 or wider, within the bound.
A program may use at most 192 MiB of HBM per device.

v0:
```python
import functools
import math

import jax
import jax.numpy as jnp
from jax import lax
from jax.sharding import PartitionSpec as P

HEADS = 12


EPSILON = 1e-06


def passed_along(block, axis, distance):
    devices = range(lax.axis_size(axis))
    route = [(i - distance, i) for i in devices if i - distance in devices]
    return lax.ppermute(block, axis, route)


def place_code(positions, model_width):
    half_width = model_width // 2
    frequency = jnp.exp(
        jnp.arange(half_width, dtype=jnp.float32) * (-math.log(10000.0) / half_width)
    )
    angles = positions.astype(jnp.float32)[..., None] * frequency
    return jnp.concatenate([jnp.sin(angles), jnp.cos(angles)], -1)


def norm_rows(values, norm_gain, norm_bias):
    row_mean = jnp.mean(values, -1, keepdims=True)
    centred = values - row_mean
    inv_std = lax.rsqrt(jnp.mean(centred * centred, -1, keepdims=True) + EPSILON)
    scaled = centred * inv_std
    return (scaled * norm_gain + norm_bias, scaled, inv_std)


def norm_back(gradient, scaled, inv_std, norm_gain):
    centred_grad = gradient * norm_gain
    centred_grad = (
        centred_grad
        - jnp.mean(centred_grad, -1, keepdims=True)
        - scaled * jnp.mean(centred_grad * scaled, -1, keepdims=True)
    )
    return (inv_std * centred_grad, jnp.sum(gradient * scaled, (0, 1)), jnp.sum(gradient, (0, 1)))


def exact_gelu(values):
    return jax.nn.gelu(values, approximate=False)


def run_if(active, branch_fn, zero_fn, *operands):
    if active is None:
        return branch_fn(*operands)
    return lax.cond(active, branch_fn, zero_fn, *operands)


def soft_scores(queries, key_rows, live_keys, head_dim, log_total):
    images, row_count, local_width = queries.shape
    key_count = key_rows.shape[1]
    head_count = local_width // head_dim
    scores = jnp.einsum(
        "iqhe,ikhe->ihqk",
        queries.reshape(images, row_count, head_count, head_dim),
        key_rows.reshape(images, key_count, head_count, head_dim),
        preferred_element_type=jnp.float32,
    ) * head_dim ** (-0.5)
    scores = jnp.where(live_keys, scores, -jnp.inf)
    if log_total is None:
        row_max = jnp.max(scores, -1, keepdims=True)
        log_total = row_max + jnp.log(jnp.sum(jnp.exp(scores - row_max), -1, keepdims=True))
    return (jnp.exp(scores - log_total), log_total)


def attend_front(normed_all, live_keys, qkv_weight, out_weight, ctx_count, head_dim):
    images, key_count, model_width = normed_all.shape
    row_count = key_count - ctx_count
    local_width = qkv_weight.shape[2]
    head_count = local_width // head_dim
    queries = jnp.einsum(
        "ikd,de->ike", normed_all[:, ctx_count:], qkv_weight[0], preferred_element_type=jnp.float32
    ).astype(jnp.bfloat16)
    key_value = jnp.einsum(
        "ikd,sde->sike", normed_all, qkv_weight[1:], preferred_element_type=jnp.float32
    ).astype(jnp.bfloat16)
    attention, log_total = soft_scores(queries, key_value[0], live_keys, head_dim, None)
    mixture = jnp.einsum(
        "ihqk,ikhe->iqhe",
        attention.astype(jnp.bfloat16),
        key_value[1].reshape(images, key_count, head_count, head_dim),
        preferred_element_type=jnp.float32,
    )
    mixture = mixture.reshape(images, row_count, local_width).astype(jnp.bfloat16)
    partial_out = jnp.einsum("iqe,ed->iqd", mixture, out_weight, preferred_element_type=jnp.float32)
    return (partial_out, queries, key_value, log_total, mixture)


def attend_zero(normed_all, live_keys, qkv_weight, out_weight, ctx_count, head_dim):
    images, key_count, model_width = normed_all.shape
    row_count = key_count - ctx_count
    local_width = qkv_weight.shape[2]
    head_count = local_width // head_dim
    return (
        jnp.zeros((images, row_count, model_width), jnp.float32),
        jnp.zeros((images, row_count, local_width), jnp.bfloat16),
        jnp.zeros((2, images, key_count, local_width), jnp.bfloat16),
        jnp.zeros((images, head_count, row_count, 1), jnp.float32),
        jnp.zeros((images, row_count, local_width), jnp.bfloat16),
    )


def attend_back(
    grad_rows,
    normed_all,
    queries,
    key_value,
    log_total,
    mixture,
    live_keys,
    qkv_weight,
    out_weight,
    ctx_count,
    head_dim,
):
    images, key_count, model_width = normed_all.shape
    row_count = key_count - ctx_count
    local_width = qkv_weight.shape[2]
    head_count = local_width // head_dim
    factor = head_dim ** (-0.5)
    out_grad = jnp.einsum("iqe,iqd->ed", mixture, grad_rows, preferred_element_type=jnp.float32)
    mixture_grad = jnp.einsum(
        "iqd,ed->iqe", grad_rows, out_weight, preferred_element_type=jnp.float32
    ).astype(jnp.bfloat16)
    mixture_grad = mixture_grad.reshape(images, row_count, head_count, head_dim)
    attention, log_total = soft_scores(queries, key_value[0], live_keys, head_dim, log_total)
    value_heads = key_value[1].reshape(images, key_count, head_count, head_dim)
    value_grad = jnp.einsum(
        "ihqk,iqhe->ikhe",
        attention.astype(jnp.bfloat16),
        mixture_grad,
        preferred_element_type=jnp.float32,
    )
    attention_grad = jnp.einsum(
        "iqhe,ikhe->ihqk", mixture_grad, value_heads, preferred_element_type=jnp.float32
    )
    score_grad = attention * (
        attention_grad - jnp.sum(attention * attention_grad, -1, keepdims=True)
    )
    score_grad = score_grad.astype(jnp.bfloat16)
    query_grad = (
        jnp.einsum(
            "ihqk,ikhe->iqhe",
            score_grad,
            key_value[0].reshape(images, key_count, head_count, head_dim),
            preferred_element_type=jnp.float32,
        )
        * factor
    )
    key_grad = (
        jnp.einsum(
            "ihqk,iqhe->ikhe",
            score_grad,
            queries.reshape(images, row_count, head_count, head_dim),
            preferred_element_type=jnp.float32,
        )
        * factor
    )
    query_grad = query_grad.reshape(images, row_count, local_width).astype(jnp.bfloat16)
    pair_grad = jnp.stack(
        [
            key_grad.reshape(images, key_count, local_width),
            value_grad.reshape(images, key_count, local_width),
        ]
    ).astype(jnp.bfloat16)
    weight_query = jnp.einsum(
        "ikd,ike->de", normed_all[:, ctx_count:], query_grad, preferred_element_type=jnp.float32
    )
    weight_pair = jnp.einsum(
        "ikd,sike->sde", normed_all, pair_grad, preferred_element_type=jnp.float32
    )
    qkv_grad = jnp.concatenate([weight_query[None], weight_pair], 0)
    partial_out = jnp.einsum(
        "sike,sde->ikd", pair_grad, qkv_weight[1:], preferred_element_type=jnp.float32
    )
    partial_out = partial_out.at[:, ctx_count:].add(
        jnp.einsum("iqe,de->iqd", query_grad, qkv_weight[0], preferred_element_type=jnp.float32)
    )
    return (partial_out, qkv_grad, out_grad)


def attend_back_zero(
    grad_rows,
    normed_all,
    queries,
    key_value,
    log_total,
    mixture,
    live_keys,
    qkv_weight,
    out_weight,
    ctx_count,
    head_dim,
):
    images, key_count, model_width = normed_all.shape
    local_width = qkv_weight.shape[2]
    return (
        jnp.zeros((images, key_count, model_width), jnp.float32),
        jnp.zeros((3, model_width, local_width), jnp.float32),
        jnp.zeros((local_width, model_width), jnp.float32),
    )


def mlp_front(normed_two, up_weight, up_bias, down_weight):
    pre_act = jnp.einsum(
        "iqd,df->iqf", normed_two, up_weight, preferred_element_type=jnp.float32
    ) + up_bias.astype(jnp.float32)
    activation = exact_gelu(pre_act).astype(jnp.bfloat16)
    partial_out = jnp.einsum(
        "iqf,fd->iqd", activation, down_weight, preferred_element_type=jnp.float32
    )
    return (partial_out, pre_act, activation)


def mlp_zero(normed_two, up_weight, up_bias, down_weight):
    images, row_count, model_width = normed_two.shape
    hidden_width = up_weight.shape[1]
    return (
        jnp.zeros((images, row_count, model_width), jnp.float32),
        jnp.zeros((images, row_count, hidden_width), jnp.float32),
        jnp.zeros((images, row_count, hidden_width), jnp.bfloat16),
    )


def mlp_back(grad_rows, normed_two, pre_act, activation, up_weight, down_weight):
    down_grad = jnp.einsum("iqf,iqd->fd", activation, grad_rows, preferred_element_type=jnp.float32)
    act_grad = jnp.einsum("iqd,fd->iqf", grad_rows, down_weight, preferred_element_type=jnp.float32)
    pre_grad = jax.vjp(exact_gelu, pre_act)[1](act_grad)[0]
    bias_grad = jnp.sum(pre_grad, (0, 1))
    pre_grad = pre_grad.astype(jnp.bfloat16)
    up_grad = jnp.einsum("iqd,iqf->df", normed_two, pre_grad, preferred_element_type=jnp.float32)
    partial_out = jnp.einsum("iqf,df->iqd", pre_grad, up_weight, preferred_element_type=jnp.float32)
    return (partial_out, up_grad, bias_grad, down_grad)


def mlp_back_zero(grad_rows, normed_two, pre_act, activation, up_weight, down_weight):
    images, row_count, model_width = normed_two.shape
    hidden_width = up_weight.shape[1]
    return (
        jnp.zeros((images, row_count, model_width), jnp.float32),
        jnp.zeros((model_width, hidden_width), jnp.float32),
        jnp.zeros((hidden_width,), jnp.float32),
        jnp.zeros((hidden_width, model_width), jnp.float32),
    )


def forward_pass(active, rows_own, ctx_count, live_keys, params, head_dim):
    (
        gain_rows,
        biases,
        scales,
        qkv_weight,
        out_weight,
        up_weight,
        up_bias,
        down_weight,
        down_bias,
    ) = params
    normed, scaled_one, inv_one = norm_rows(rows_own, gain_rows[0], biases[0])
    normed_all = lax.all_gather(normed.astype(jnp.bfloat16), "head", axis=0, tiled=True)
    qkv_use, out_use = (qkv_weight, out_weight)
    front_fn = functools.partial(
        attend_front, qkv_weight=qkv_use, out_weight=out_use, ctx_count=ctx_count, head_dim=head_dim
    )
    front_zero = functools.partial(
        attend_zero, qkv_weight=qkv_use, out_weight=out_use, ctx_count=ctx_count, head_dim=head_dim
    )
    partial_out, queries, key_value, log_total, mixture = run_if(
        active, front_fn, front_zero, normed_all, live_keys
    )
    attended = lax.psum_scatter(
        partial_out.astype(jnp.bfloat16), "head", scatter_dimension=0, tiled=True
    ).astype(jnp.float32)
    hidden = rows_own[:, ctx_count:] + scales[0] * attended
    normed_two, scaled_two, inv_two = norm_rows(hidden, gain_rows[1], biases[1])
    normed_two = normed_two.astype(jnp.bfloat16)
    normed_two = lax.all_gather(normed_two, "head", axis=0, tiled=True)
    feed_fn = functools.partial(
        mlp_front, up_weight=up_weight, up_bias=up_bias, down_weight=down_weight
    )
    feed_zero = functools.partial(
        mlp_zero, up_weight=up_weight, up_bias=up_bias, down_weight=down_weight
    )
    mlp_out, pre_act, activation = run_if(active, feed_fn, feed_zero, normed_two)
    mlp_out = lax.psum_scatter(
        mlp_out.astype(jnp.bfloat16), "head", scatter_dimension=0, tiled=True
    ).astype(jnp.float32)
    branch_out = mlp_out + down_bias
    result = hidden + scales[1] * branch_out
    kept = (
        scaled_one,
        inv_one,
        normed_all,
        queries,
        key_value,
        log_total,
        mixture,
        attended,
        scaled_two,
        inv_two,
        normed_two,
        pre_act,
        activation,
        branch_out,
    )
    return (result, kept)


def backward_pass(active, output_grad, kept, ctx_count, live_keys, params, head_dim):
    (
        gain_rows,
        biases,
        scales,
        qkv_weight,
        out_weight,
        up_weight,
        up_bias,
        down_weight,
        down_bias,
    ) = params
    (
        scaled_one,
        inv_one,
        normed_all,
        queries,
        key_value,
        log_total,
        mixture,
        attended,
        scaled_two,
        inv_two,
        normed_two,
        pre_act,
        activation,
        branch_out,
    ) = kept
    branch_grad = scales[1] * output_grad
    scale_two_grad = jnp.sum(output_grad * branch_out, (0, 1))
    down_bias_grad = jnp.sum(branch_grad, (0, 1))
    branch_grad = branch_grad.astype(jnp.bfloat16)
    branch_grad = lax.all_gather(branch_grad, "head", axis=0, tiled=True)
    back_fn = functools.partial(mlp_back, up_weight=up_weight, down_weight=down_weight)
    back_zero = functools.partial(mlp_back_zero, up_weight=up_weight, down_weight=down_weight)
    partial_out, up_grad, up_bias_grad, down_grad = run_if(
        active, back_fn, back_zero, branch_grad, normed_two, pre_act, activation
    )
    normed_two_grad = lax.psum_scatter(
        partial_out.astype(jnp.bfloat16), "head", scatter_dimension=0, tiled=True
    ).astype(jnp.float32)
    hidden_grad, gain_two_grad, bias_two_grad = norm_back(
        normed_two_grad, scaled_two, inv_two, gain_rows[1]
    )
    hidden_grad = output_grad + hidden_grad
    scale_one_grad = jnp.sum(hidden_grad * attended, (0, 1))
    attended_grad = (scales[0] * hidden_grad).astype(jnp.bfloat16)
    attended_grad = lax.all_gather(attended_grad, "head", axis=0, tiled=True)
    qkv_use, out_use = (qkv_weight, out_weight)
    attend_fn = functools.partial(
        attend_back, qkv_weight=qkv_use, out_weight=out_use, ctx_count=ctx_count, head_dim=head_dim
    )
    attend_zero_fn = functools.partial(
        attend_back_zero,
        qkv_weight=qkv_use,
        out_weight=out_use,
        ctx_count=ctx_count,
        head_dim=head_dim,
    )
    partial_out, qkv_grad, out_grad = run_if(
        active,
        attend_fn,
        attend_zero_fn,
        attended_grad,
        normed_all,
        queries,
        key_value,
        log_total,
        mixture,
        live_keys,
    )
    normed_grad = lax.psum_scatter(
        partial_out.astype(jnp.bfloat16), "head", scatter_dimension=0, tiled=True
    ).astype(jnp.float32)
    rows_grad, gain_one_grad, bias_one_grad = norm_back(
        normed_grad, scaled_one, inv_one, gain_rows[0]
    )
    vectors = (
        jnp.stack([gain_one_grad, gain_two_grad]),
        jnp.stack([bias_one_grad, bias_two_grad]),
        jnp.stack([scale_one_grad, scale_two_grad]),
        down_bias_grad,
    )
    matrices = (qkv_grad, out_grad, up_grad, up_bias_grad, down_grad)
    return (rows_grad, hidden_grad, vectors, matrices)


def shards(
    patches,
    order,
    cotangent,
    norm_gains,
    norm_biases,
    layer_scales,
    qkv_weight,
    out_weight,
    up_weight,
    up_bias,
    down_weight,
    down_bias,
    mask_token,
):
    params = (
        norm_gains[0],
        norm_biases[0],
        layer_scales[0],
        qkv_weight[0],
        out_weight[0],
        up_weight[0],
        up_bias[0],
        down_weight[0],
        down_bias[0],
    )
    images, npatch, model_width = patches.shape
    visible_count = npatch // 2
    head_dim = model_width // HEADS
    encoder = lax.axis_index("stream") == 0
    regressor = jnp.logical_not(encoder)
    visible = order[:, :visible_count]
    masked = order[:, visible_count:]
    seen_rows = jnp.take_along_axis(patches, visible[..., None], 1).astype(jnp.float32)
    masked_rows = jnp.take_along_axis(patches, masked[..., None], 1).astype(jnp.float32)
    all_live = jnp.ones((visible_count,), jnp.bool_)
    latent, kept_first = forward_pass(encoder, seen_rows, 0, all_live, params, head_dim)
    latent = latent.astype(jnp.bfloat16)
    arrived = passed_along(latent, "stream", 1)
    context_live = jnp.concatenate([jnp.broadcast_to(regressor, (visible_count,)), all_live])
    context = arrived.astype(jnp.float32) + place_code(visible, model_width)
    queries = mask_token + place_code(masked, model_width)
    rows_second = jnp.where(
        encoder,
        jnp.concatenate([jnp.zeros_like(context), masked_rows], 1),
        jnp.concatenate([context, queries], 1),
    )
    produced, kept_second = forward_pass(
        None, rows_second, visible_count, context_live, params, head_dim
    )
    output_grad = cotangent[0].astype(jnp.float32)
    rows_grad, hidden_grad, vectors_reg, matrices_reg = backward_pass(
        regressor, output_grad, kept_second, visible_count, context_live, params, head_dim
    )
    context_grad = rows_grad[:, :visible_count]
    query_grad = hidden_grad + rows_grad[:, visible_count:]
    returned = passed_along(context_grad.astype(jnp.bfloat16), "stream", -1)
    latent_grad = output_grad + returned.astype(jnp.float32)
    seen_grad, seen_hidden_grad, vectors_enc, matrices_enc = backward_pass(
        encoder, latent_grad, kept_first, 0, all_live, params, head_dim
    )
    seen_grad = seen_grad + seen_hidden_grad

    def spread_rows(positions, values):
        return jnp.zeros((npatch, model_width), jnp.float32).at[positions].set(values)

    patch_grad = jax.vmap(spread_rows)(visible, seen_grad)
    input_grad = jnp.where(encoder, patch_grad, jnp.concatenate([context_grad, query_grad], 1))

    def pick_own(enc_value, reg_value):
        return jnp.where(encoder, enc_value, reg_value)

    matrices = jax.tree.map(pick_own, matrices_enc, matrices_reg)
    vectors = jax.tree.map(pick_own, vectors_enc, vectors_reg)
    matrices = lax.psum(matrices, "dp")

    def both_slots(values):
        zero_values = jnp.zeros_like(values)
        return jnp.stack(
            [jnp.where(encoder, values, zero_values), jnp.where(encoder, zero_values, values)]
        )

    token_part = jnp.where(
        encoder, jnp.zeros((model_width,), jnp.float32), jnp.sum(query_grad, (0, 1))
    )
    totals = lax.psum(
        (
            both_slots(vectors[0]),
            both_slots(vectors[1]),
            both_slots(vectors[2]),
            both_slots(vectors[3]),
            token_part,
        ),
        ("stream", "dp", "head"),
    )

    def own_slot(stacked):
        return jnp.where(encoder, stacked[0], stacked[1])[None]

    return (
        jnp.where(encoder, latent, arrived),
        produced.astype(jnp.bfloat16)[None],
        input_grad[None],
        own_slot(totals[0]),
        own_slot(totals[1]),
        own_slot(totals[2]),
        matrices[0][None],
        matrices[1][None],
        matrices[2][None],
        matrices[3][None],
        matrices[4][None],
        own_slot(totals[3]),
        totals[4],
    )


def solution(mesh):
    in_specs = (
        P(("dp", "head"), None, None),
        P(("dp", "head"), None),
        P("stream", ("dp", "head"), None, None),
        P("stream", None, None),
        P("stream", None, None),
        P("stream", None, None),
        P("stream", None, None, "head"),
        P("stream", "head", None),
        P("stream", None, "head"),
        P("stream", "head"),
        P("stream", "head", None),
        P("stream", None),
        P(),
    )
    out_specs = (
        P(("dp", "head"), None, None),
        P("stream", ("dp", "head"), None, None),
        P("stream", ("dp", "head"), None, None),
        P("stream", None, None),
        P("stream", None, None),
        P("stream", None, None),
        P("stream", None, None, "head"),
        P("stream", "head", None),
        P("stream", None, "head"),
        P("stream", "head"),
        P("stream", "head", None),
        P("stream", None),
        P(),
    )
    return jax.shard_map(shards, mesh=mesh, in_specs=in_specs, out_specs=out_specs, check_vma=False)
```

profile of v0, /device:TPU:0, one launch (start us, length us, event | category | flops | bytes accessed | tf_op | source)
XLA Modules:
  0.0 1050.6 jit_solution(8578484846499390923)
XLA Ops:
  9.4 4.7 gather_fusion
  16.6 12.6 %all-gather.9.cloned.1.call-done = bf16[4,256,768]{2,1,0:T(8,128)(2,1)} async-done(((bf16[2,256,768]{2,1,0:T(8,128)(2,1)}), bf16[4,256,768]{2,1,0:T(8,128)(2,1)}) %all-gather.9.cloned.1.call-update) | async-done | bytes 1572880 | tf_op jit(solution)/shard_map/all_gather | solution.py:269
  29.2 24.5 %conditional.6 = (bf16[4,256,768]{2,1,0:T(8,128)(2,1)}, bf16[4,256,384]{2,1,0:T(8,128)(2,1)S(1)}, bf16[2,4,256,384]{2,3,1,0:T(8,128)(2,1)}, f32[4,6,256,1]{2,1,0,3:T(8,128)}, bf16[4,256,384]{1,2,0:T(8,128)(2,1)}) conditional(s32[]{:T(128)} %convert_element_type.229, () %tuple.68, (bf16[3,768,384]{2,1,0:T(8,128)(2,1)}, bf16[4,256,768]{2,1,0:T(8,128)(2,1)}, ...), branch_computations={%region_2.0_spmd, %region_3.7_spmd} | conditional | flops 2832721920 | bytes 58761396 | solution.py:55
  33.0 4.4 fusion.4
  54.7 8.5 reduce-scatter.9.cloned.1.call-done
  68.2 11.2 %all-gather.11.cloned.1.call-done = bf16[4,256,768]{2,1,0:T(8,128)(2,1)} async-done(((bf16[2,256,768]{2,1,0:T(8,128)(2,1)}), bf16[4,256,768]{2,1,0:T(8,128)(2,1)}) %all-gather.11.cloned.1.call-update) | async-done | bytes 1572880 | tf_op jit(solution)/shard_map/all_gather | solution.py:286
  79.4 25.5 %conditional.7 = (bf16[4,256,768]{2,1,0:T(8,128)(2,1)}, f32[4,256,1536]{2,1,0:T(8,128)}, bf16[4,256,1536]{2,1,0:T(8,128)(2,1)}) conditional(s32[]{:T(128)} %convert_element_type.229, () %tuple.70, (bf16[4,256,768]{2,1,0:T(8,128)(2,1)}, bf16[768,1536]{1,0:T(8,128)(2,1)}, bf16[1,1536]{1,0:T(2,128)(2,1)S(1)}, bf16[1536,768]{1,0:T(8,128)(2,1)}) %tuple.221), branch_computations={%region_9.11_spmd, %region_10.12_spmd} | conditional | flops 4935648768 | bytes 29899828 | solution.py:55
  79.6 19.6 %fusion.95 = (bf16[4,256,1536]{2,1,0:T(8,128)(2,1)}, f32[4,256,1536]{2,1,0:T(8,128)}) fusion(f32[1536]{0:T(1024)S(1)} %convert_reduce_fusion, bf16[4,256,768]{2,1,0:T(8,128)(2,1)} %get-tuple-element.117, bf16[768,1536]{1,0:T(8,128)(2,1)} %get-tuple-element.118), kind=kOutput, calls=%fused_computation.140 | convolution fusion | flops 2519728128 | bytes 13375488 | tf_op jit(solution)/shard_map/cond/branch_1_fun/iqd,df->iqf/dot_general | solution.py:214
  99.2 5.6 fusion.103
  104.9 7.2 gather_fusion.1
  121.3 5.5 multiply_sine_fusion.1
  127.0 11.1 %collective-permute-done = bf16[2,256,768]{2,1,0:T(8,128)(2,1)S(1)} collective-permute-done((bf16[2,256,768]{2,1,0:T(8,128)(2,1)S(1)}, bf16[2,256,768]{2,1,0:T(8,128)(2,1)S(1)}, u32[]{:S(2)}, u32[]{:S(2)}) %collective-permute-start) | collective-permute-done | bytes 786464 | tf_op jit(solution)/shard_map/ppermute | solution.py:18
  143.3 13.8 %all-gather.13.cloned.1.call-done = bf16[4,512,768]{2,1,0:T(8,128)(2,1)} async-done(((bf16[2,512,768]{2,1,0:T(8,128)(2,1)}), bf16[4,512,768]{2,1,0:T(8,128)(2,1)}) %all-gather.13.cloned.1.call-update) | async-done | bytes 3145744 | tf_op jit(solution)/shard_map/all_gather | solution.py:269
  157.1 4.8 convert_bitcast_fusion
  180.9 10.3 reduce-scatter.13.cloned.1.call-done
  196.0 10.0 all-gather.15.cloned.1.call-done
  206.0 6.1 fusion.175
  214.7 14.9 %fusion.109 = bf16[4,256,1536]{2,1,0:T(8,128)(2,1)} fusion(f32[4,256,1536]{2,1,0:T(8,128)S(1)} %get-tuple-element.421, u8[256,1536]{1,0:T(8,128)(4,1)S(1)} %get-tuple-element.327, u8[256,1536]{1,0:T(8,128)(4,1)S(1)} %get-tuple-element.326), kind=kLoop, calls=%fused_computation.168 | loop fusion | flops 110100480 | bytes 10223616 | tf_op jit(solution)/shard_map/convert_element_type | solution.py:217
  229.6 5.6 conditional.8
  236.4 6.4 fusion.148
  243.1 39.7 %reduce-scatter.17.cloned.1.call-done = bf16[2,256,768]{2,1,0:T(8,128)(2,1)} async-done(((bf16[4,256,768]{2,1,0:T(8,128)(2,1)}), bf16[2,256,768]{2,1,0:T(8,128)(2,1)}) %reduce-scatter.17.cloned.1.call-update) | async-done | bytes 786448 | tf_op jit(solution)/shard_map/reduce_scatter | solution.py:356
  285.3 9.9 reduce-scatter.15.cloned.1.call-done
  301.3 11.2 %all-gather.19.cloned.1.call-done = bf16[4,256,768]{2,1,0:T(8,128)(2,1)} async-done(((bf16[2,256,768]{2,1,0:T(8,128)(2,1)}), bf16[4,256,768]{2,1,0:T(8,128)(2,1)}) %all-gather.19.cloned.1.call-update) | async-done | bytes 1572880 | tf_op jit(solution)/shard_map/all_gather | solution.py:365
  312.5 8.9 conditional.9
  321.4 5.2 convert_element_type.263
  326.8 86.7 %reduce-scatter.19.cloned.1.call-done = bf16[2,512,768]{2,1,0:T(8,128)(2,1)} async-done(((bf16[4,512,768]{2,1,0:T(8,128)(2,1)}), bf16[2,512,768]{2,1,0:T(8,128)(2,1)}) %reduce-scatter.19.cloned.1.call-update) | async-done | bytes 1572880 | tf_op jit(solution)/shard_map/reduce_scatter | solution.py:389
  422.4 20.4 %collective-permute-done.1 = bf16[2,256,768]{2,1,0:T(8,128)(2,1)S(1)} collective-permute-done((bf16[2,256,768]{2,1,0:T(8,128)(2,1)S(1)}, bf16[2,256,768]{2,1,0:T(8,128)(2,1)S(1)}, u32[]{:S(2)}, u32[]{:S(2)}) %collective-permute-start.1) | collective-permute-done | bytes 786464 | tf_op jit(solution)/shard_map/ppermute | solution.py:18
  444.6 10.1 all-gather.21.cloned.1.call-done
  454.7 45.1 %conditional.10 = (bf16[4,256,768]{2,1,0:T(8,128)(2,1)}, f32[1536]{0:T(1024)S(1)}, f32[1536,768]{1,0:T(8,128)}, f32[768,1536]{1,0:T(8,128)}) conditional(s32[]{:T(128)} %convert_element_type.229, () %tuple.77, (f32[4,256,1536]{2,1,0:T(8,128)}, bf16[4,256,768]{2,1,0:T(8,128)(2,1)}, bf16[1536,768]{1,0:T(8,128)(2,1)}, bf16[768,1536]{1,0:T(8,128)(2,1)}, ...), branch_computations={%region_32.34_spmd, %region_33.36_spmd} | conditional | flops 9778493440 | bytes 73930864 | solution.py:55
  454.9 19.6 %fusion.201 = (f32[1536]{0:T(1024)S(1)}, bf16[4,256,1536]{2,1,0:T(8,128)(2,1)S(1)}) fusion(f32[4,256,1536]{2,1,0:T(8,128)} %get-tuple-element.137, bf16[4,256,768]{2,1,0:T(8,128)(2,1)} %get-tuple-element.138, bf16[1536,768]{1,0:T(8,128)(2,1)} %get-tuple-element.139), kind=kOutput, calls=%fused_computation.384 | convolution fusion | flops 2530736640 | bytes 13375488 | tf_op jit(solution)/shard_map/cond/branch_1_fun/iqd,fd->iqf/dot_general | solution.py:236
  476.1 4.3 convolution_bitcast_fusion.5
  480.4 6.1 copy.152
  486.5 6.5 fusion.70
  493.0 6.8 convolution_bitcast_fusion.4
  500.1 9.2 reduce-scatter.21.cloned.1.call-done
  516.5 11.2 %all-gather.23.cloned.1.call-done = bf16[4,256,768]{2,1,0:T(8,128)(2,1)} async-done(((bf16[2,256,768]{2,1,0:T(8,128)(2,1)}), bf16[4,256,768]{2,1,0:T(8,128)(2,1)}) %all-gather.23.cloned.1.call-update) | async-done | bytes 1572880 | tf_op jit(solution)/shard_map/all_gather | solution.py:365
  527.7 49.1 %conditional.11 = (bf16[4,256,768]{2,1,0:T(8,128)(2,1)}, f32[384,768]{1,0:T(8,128)}, f32[3,768,384]{2,1,0:T(8,128)}) conditional(s32[]{:T(128)} %convert_element_type.229, () %tuple.72, (bf16[4,256,384]{2,1,0:T(8,128)(2,1)S(1)}, bf16[2,4,256,384]{2,3,1,0:T(8,128)(2,1)}, f32[4,6,256,1]{2,1,0,3:T(8,128)}, bf16[4,256,768]{2,1,0:T(8,128)(2,1)}, ...), branch_computations={%region_38.40_spmd, %region_39.42_spmd} | conditional | flops 5863729152 | bytes 187294112 | solution.py:55
  536.5 5.1 multiply_reduce_fusion.2
  561.9 5.6 copy.154
  576.9 5.1 select_bitcast_fusion
  582.0 6.1 select_bitcast_fusion.1
  590.6 4.2 select_bitcast_fusion.2
  601.3 24.0 %psum.76 = f32[1,1536]{1,0:T(1,128)} all-reduce(f32[1,1536]{1,0:T(1,128)S(1)} %broadcast_in_dim.117), channel_id=1, replica_groups=mesh['stream'=2,'dp'=8,'head'=2] {'dp'}, use_global_device_ids=true, to_apply=%region_63.65 | all-reduce | flops 1536 | bytes 12288 | tf_op jit(solution)/shard_map/psum | solution.py:479
  632.5 69.6 %scatter_fusion = f32[2,512,768]{2,1,0:T(8,128)} fusion(f32[2,512,768]{2,1,0:T(8,128)} %broadcast_in_dim.69, s32[512]{0:T(512)S(1)} %bitcast.327, f32[512,768]{1,0:T(8,128)} %bitcast.342), kind=kCustom, calls=%fused_computation.2 | custom fusion | bytes 4722688 | tf_op jit(solution)/shard_map/vmap()/scatter | solution.py:469
  702.2 43.1 %all-reduce.2 = (f32[2,2,768]{2,1,0:T(2,128)S(1)}, f32[2,2,768]{2,1,0:T(2,128)S(1)}, f32[2,2,768]{2,1,0:T(2,128)S(1)}, f32[2,768]{1,0:T(2,128)S(1)}, f32[768]{0:T(1024)}) all-reduce(f32[2,2,768]{2,1,0:T(2,128)S(1)} %pad_maximum_fusion.10, ...), channel_id=1, replica_groups=mesh['stream'=2,'dp'=8,'head'=2] {'stream','dp','head'}, use_global_device_ids=true, to_apply=%region_49.51 | all-reduce | flops 11520 | bytes 92160 | tf_op jit(solution)/shard_map/psum | solution.py:490
  747.1 4.4 fusion.125
  751.5 281.2 %all-reduce.6.cloned.1.call-done = (f32[1,3,768,384]{3,2,1,0:T(8,128)}, f32[1,384,768]{2,1,0:T(8,128)}, f32[1,768,1536]{2,1,0:T(8,128)}, f32[1,1536,768]{2,1,0:T(8,128)}) async-done(((f32[1,3,768,384]{3,2,1,0:T(8,128)}, f32[1,384,768]{2,1,0:T(8,128)}, f32[1,768,1536]{2,1,0:T(8,128)}, f32[1,1536,768]{2,1,0:T(8,128)}), (f32[1,3,768,384]{3,2,1,0:T(8,128)}, f32[1,384,768]{2,1,0:T(8,128)}, ...) | async-done | bytes 14155792 | tf_op jit(solution)/shard_map/psum | solution.py:479
  1032.7 4.2 copy.211
  (365 shorter events, 173.7 us)
Async XLA Ops:
  7.2 22.0 %all-gather.9.cloned.1.call-start = ((), (), s32[]{:S(2)}) async-start(), calls=%async_computation.8 | async-start | bytes 2359296 | tf_op jit(solution)/shard_map/all_gather | solution.py:269
  9.3 105.1 %copy-start.51 = (pred[2,256]{1,0:T(4,128)(4,1)}, pred[2,256]{1,0:T(4,128)(4,1)S(1)}, u32[]{:S(2)}) copy-start(pred[2,256]{1,0:T(4,128)(4,1)S(1)} %get-tuple-element.410) | copy-start | bytes 1540
  14.1 100.4 %copy-start.2 = (bf16[512,768]{1,0:T(8,128)(2,1)}, bf16[512,768]{1,0:T(8,128)(2,1)S(1)}, u32[]{:S(2)}) copy-start(bf16[512,768]{1,0:T(8,128)(2,1)S(1)} %gather_fusion) | copy-start | bytes 2359300
  14.4 14.8 %copy-start.57 = (f32[2,256]{1,0:T(2,128)}, f32[2,256]{1,0:T(2,128)S(1)}, u32[]{:S(2)}) copy-start(f32[2,256]{1,0:T(2,128)S(1)} %broadcast_multiply_fusion.11) | copy-start | bytes 6148
  14.9 14.3 %copy-start.64 = (f32[2,256]{1,0:T(2,128)}, f32[2,256]{1,0:T(2,128)S(1)}, u32[]{:S(2)}) copy-start(f32[2,256]{1,0:T(2,128)S(1)} %add_rsqrt_fusion.3) | copy-start | bytes 6148
  14.9 125.2 %copy-start.49 = (f32[768]{0:T(1024)}, f32[768]{0:T(1024)S(1)}, u32[]{:S(2)}) copy-start(f32[768]{0:T(1024)S(1)} %get-tuple-element.350) | copy-start | bytes 9220
  16.5 46.7 %reduce-scatter.9.cloned.1.call-start = ((), (), s32[]{:S(2)}) async-start(), calls=%async_computation.9 | async-start | bytes 2359296 | tf_op jit(solution)/shard_map/reduce_scatter | solution.py:280
  29.2 24.6 %copy-start.75 = (f32[1,2,768]{2,1,0:T(2,128)S(1)}, f32[1,2,768]{2,1,0:T(2,128)}, u32[]{:S(2)}) copy-start(f32[1,2,768]{2,1,0:T(2,128)} %param.38) | copy-start | bytes 18436
  53.8 25.6 %all-gather.11.cloned.1.call-start = ((), (), s32[]{:S(2)}) async-start(), calls=%async_computation.10 | async-start | bytes 2359296 | tf_op jit(solution)/shard_map/all_gather | solution.py:286
  63.2 16.2 %copy-start.68 = (bf16[1,1536]{1,0:T(2,128)(2,1)S(1)}, bf16[1,1536]{1,0:T(2,128)(2,1)}, u32[]{:S(2)}) copy-start(bf16[1,1536]{1,0:T(2,128)(2,1)} %param.42) | copy-start | bytes 9220
  64.9 14.5 %copy-start.59 = (f32[2,256]{1,0:T(2,128)}, f32[2,256]{1,0:T(2,128)S(1)}, u32[]{:S(2)}) copy-start(f32[2,256]{1,0:T(2,128)S(1)} %broadcast_multiply_fusion.10) | copy-start | bytes 6148
  66.6 12.7 %copy-start.66 = (f32[2,256]{1,0:T(2,128)}, f32[2,256]{1,0:T(2,128)S(1)}, u32[]{:S(2)}) copy-start(f32[2,256]{1,0:T(2,128)S(1)} %add_rsqrt_fusion.2) | copy-start | bytes 6148
  68.1 46.3 %reduce-scatter.11.cloned.1.call-start = ((), (), s32[]{:S(2)}) async-start(), calls=%async_computation.11 | async-start | bytes 2359296 | tf_op jit(solution)/shard_map/reduce_scatter | solution.py:294
  79.6 19.6 %copy-start.80 = (bf16[1536,768]{1,0:T(8,128)(2,1)S(1)}, bf16[1536,768]{1,0:T(8,128)(2,1)}, u32[]{:S(2)}) copy-start(bf16[1536,768]{1,0:T(8,128)(2,1)} %get-tuple-element.120) | copy-start | bytes 7077892 | tf_op jit(solution)/shard_map/cond
  104.9 52.2 %all-gather.13.cloned.1.call-start = ((), (), s32[]{:S(2)}) async-start(), calls=%async_computation.12 | async-start | bytes 4718592 | tf_op jit(solution)/shard_map/all_gather | solution.py:269
  117.4 20.8 %collective-permute-start = (bf16[2,256,768]{2,1,0:T(8,128)(2,1)S(1)}, bf16[2,256,768]{2,1,0:T(8,128)(2,1)S(1)}, u32[]{:S(2)}, u32[]{:S(2)}) collective-permute-start(bf16[2,256,768]{2,1,0:T(8,128)(2,1)S(1)} %get-tuple-element.405), channel_id=1, source_target_pairs={{0,16},{1,17},{2,18},{3,19},{4,20},{5,21},{6,22},{7,23},{8,24},{9,... | collective-permute-start | bytes 2359304 | tf_op jit(solution)/shard_map/ppermute | solution.py:18
  141.2 15.9 %copy-start.28 = (bf16[1,3,768,384]{3,2,1,0:T(8,128)(2,1)S(1)}, bf16[1,3,768,384]{3,2,1,0:T(8,128)(2,1)}, u32[]{:S(2)}) copy-start(bf16[1,3,768,384]{3,2,1,0:T(8,128)(2,1)} %param.39) | copy-start | bytes 5308420
  142.9 48.3 %reduce-scatter.13.cloned.1.call-start = ((), (), s32[]{:S(2)}) async-start(), calls=%async_computation.13 | async-start | bytes 2359296 | tf_op jit(solution)/shard_map/reduce_scatter | solution.py:280
  180.9 25.1 %all-gather.15.cloned.1.call-start = ((), (), s32[]{:S(2)}) async-start(), calls=%async_computation.14 | async-start | bytes 2359296 | tf_op jit(solution)/shard_map/all_gather | solution.py:286
  194.7 34.9 %all-gather.17.cloned.1.call-start = ((), (), s32[]{:S(2)}) async-start(), calls=%async_computation.16 | async-start | bytes 2359296 | tf_op jit(solution)/shard_map/all_gather | solution.py:350
  195.5 87.3 %reduce-scatter.17.cloned.1.call-start = ((), (), s32[]{:S(2)}) async-start(), calls=%async_computation.17 | async-start | bytes 2359296 | tf_op jit(solution)/shard_map/reduce_scatter | solution.py:356
  236.4 58.9 %reduce-scatter.15.cloned.1.call-start = ((), (), s32[]{:S(2)}) async-start(), calls=%async_computation.15 | async-start | bytes 2359296 | tf_op jit(solution)/shard_map/reduce_scatter | solution.py:294
  242.8 52.4 %copy-start.16 = (bf16[1,2,256,768]{3,2,1,0:T(8,128)(2,1)S(1)}, bf16[1,2,256,768]{3,2,1,0:T(8,128)(2,1)}, u32[]{:S(2)}) copy-start(bf16[1,2,256,768]{3,2,1,0:T(8,128)(2,1)} %param.35) | copy-start | bytes 2359300
  242.8 52.4 %copy-start.37 = (bf16[2,256,768]{2,1,0:T(8,128)(2,1)S(1)}, bf16[2,256,768]{2,1,0:T(8,128)(2,1)}, u32[]{:S(2)}) copy-start(bf16[2,256,768]{2,1,0:T(8,128)(2,1)} %reduce-scatter.13.cloned.1.call-done) | copy-start | bytes 2359300
  242.9 69.6 %all-gather.19.cloned.1.call-start = ((), (), s32[]{:S(2)}) async-start(), calls=%async_computation.18 | async-start | bytes 2359296 | tf_op jit(solution)/shard_map/all_gather | solution.py:365
  301.3 112.2 %reduce-scatter.19.cloned.1.call-start = ((), (), s32[]{:S(2)}) async-start(), calls=%async_computation.19 | async-start | bytes 4718592 | tf_op jit(solution)/shard_map/reduce_scatter | solution.py:389
  326.7 86.8 %copy-start.50 = (f32[768]{0:T(1024)S(1)}, f32[768]{0:T(1024)}, u32[]{:S(2)}) copy-start(f32[768]{0:T(1024)} %copy-done.49) | copy-start | bytes 9220
  326.7 86.8 %copy-start.54 = (f32[2,512]{1,0:T(2,128)S(1)}, f32[2,512]{1,0:T(2,128)}, u32[]{:S(2)}) copy-start(f32[2,512]{1,0:T(2,128)} %copy-done.53) | copy-start | bytes 12292
  326.7 86.8 %copy-start.56 = (f32[2,512]{1,0:T(2,128)S(1)}, f32[2,512]{1,0:T(2,128)}, u32[]{:S(2)}) copy-start(f32[2,512]{1,0:T(2,128)} %copy-done.55) | copy-start | bytes 12292
  326.7 128.0 %all-gather.21.cloned.1.call-start = ((), (), s32[]{:S(2)}) async-start(), calls=%async_computation.20 | async-start | bytes 2359296 | tf_op jit(solution)/shard_map/all_gather | solution.py:350
  416.8 26.0 %copy-start.39 = (bf16[2,256,768]{2,1,0:T(8,128)(2,1)S(1)}, bf16[2,256,768]{2,1,0:T(8,128)(2,1)}, u32[]{:S(2)}) copy-start(bf16[2,256,768]{2,1,0:T(8,128)(2,1)} %reduce-scatter.11.cloned.1.call-done) | copy-start | bytes 2359300
  416.8 26.0 %copy-start.40 = (bf16[2,256,768]{2,1,0:T(8,128)(2,1)S(1)}, bf16[2,256,768]{2,1,0:T(8,128)(2,1)}, u32[]{:S(2)}) copy-start(bf16[2,256,768]{2,1,0:T(8,128)(2,1)} %reduce-scatter.15.cloned.1.call-done) | copy-start | bytes 2359300
  421.1 21.7 %collective-permute-start.1 = (bf16[2,256,768]{2,1,0:T(8,128)(2,1)S(1)}, bf16[2,256,768]{2,1,0:T(8,128)(2,1)S(1)}, u32[]{:S(2)}, u32[]{:S(2)}) collective-permute-start(bf16[2,256,768]{2,1,0:T(8,128)(2,1)S(1)} %slice.302), channel_id=1, source_target_pairs={{16,0},{17,1},{18,2},{19,3},{20,4},{21,5},{22,6},{23,7},{24,8},{25... | collective-permute-start | bytes 2359304 | tf_op jit(solution)/shard_map/ppermute | solution.py:18
  444.5 64.8 %reduce-scatter.21.cloned.1.call-start = ((), (), s32[]{:S(2)}) async-start(), calls=%async_computation.21 | async-start | bytes 2359296 | tf_op jit(solution)/shard_map/reduce_scatter | solution.py:356
  454.7 54.6 %copy-start.3 = (bf16[512,768]{1,0:T(8,128)(2,1)S(1)}, bf16[512,768]{1,0:T(8,128)(2,1)}, u32[]{:S(2)}) copy-start(bf16[512,768]{1,0:T(8,128)(2,1)} %copy-done.2) | copy-start | bytes 2359300
  454.7 54.6 %copy-start.9 = (bf16[2,256,768]{2,1,0:T(8,128)(2,1)S(1)}, bf16[2,256,768]{2,1,0:T(8,128)(2,1)}, u32[]{:S(2)}) copy-start(bf16[2,256,768]{2,1,0:T(8,128)(2,1)} %reduce-scatter.9.cloned.1.call-done) | copy-start | bytes 2359300
  454.7 54.6 %copy-start.52 = (pred[2,256]{1,0:T(4,128)(4,1)S(1)}, pred[2,256]{1,0:T(4,128)(4,1)}, u32[]{:S(2)}) copy-start(pred[2,256]{1,0:T(4,128)(4,1)} %copy-done.51) | copy-start | bytes 1540
  454.7 54.6 %copy-start.60 = (f32[2,256]{1,0:T(2,128)S(1)}, f32[2,256]{1,0:T(2,128)}, u32[]{:S(2)}) copy-start(f32[2,256]{1,0:T(2,128)} %copy-done.59) | copy-start | bytes 6148
  454.7 54.6 %copy-start.67 = (f32[2,256]{1,0:T(2,128)S(1)}, f32[2,256]{1,0:T(2,128)}, u32[]{:S(2)}) copy-start(f32[2,256]{1,0:T(2,128)} %copy-done.66) | copy-start | bytes 6148
  454.9 21.2 %copy-start.83 = (bf16[4,256,768]{2,1,0:T(8,128)(2,1)S(1)}, bf16[4,256,768]{2,1,0:T(8,128)(2,1)}, u32[]{:S(2)}) copy-start(bf16[4,256,768]{2,1,0:T(8,128)(2,1)} %get-tuple-element.141) | copy-start | bytes 4718596 | tf_op jit(solution)/shard_map/cond
  499.9 27.8 %all-gather.23.cloned.1.call-start = ((), (), s32[]{:S(2)}) async-start(), calls=%async_computation.22 | async-start | bytes 2359296 | tf_op jit(solution)/shard_map/all_gather | solution.py:365
  511.9 15.8 %copy-start.20 = (bf16[4,256,384]{2,1,0:T(8,128)(2,1)S(1)}, bf16[4,256,384]{2,1,0:T(8,128)(2,1)}, u32[]{:S(2)}) copy-start(bf16[4,256,384]{2,1,0:T(8,128)(2,1)} %copy-done.19) | copy-start | bytes 2359300
  516.5 109.0 %reduce-scatter.23.cloned.1.call-start = ((), (), s32[]{:S(2)}) async-start(), calls=%async_computation.23 | async-start | bytes 2359296 | tf_op jit(solution)/shard_map/reduce_scatter | solution.py:389
  576.8 455.8 %all-reduce.6.cloned.1.call-start = ((), (), s32[]{:S(2)}) async-start(), calls=%async_computation.24 | async-start | bytes 28311552 | tf_op jit(solution)/shard_map/psum | solution.py:479
  597.2 28.3 %copy-start.58 = (f32[2,256]{1,0:T(2,128)S(1)}, f32[2,256]{1,0:T(2,128)}, u32[]{:S(2)}) copy-start(f32[2,256]{1,0:T(2,128)} %copy-done.57) | copy-start | bytes 6148
  597.2 28.3 %copy-start.65 = (f32[2,256]{1,0:T(2,128)S(1)}, f32[2,256]{1,0:T(2,128)}, u32[]{:S(2)}) copy-start(f32[2,256]{1,0:T(2,128)} %copy-done.64) | copy-start | bytes 6148
  601.2 26.5 %copy-start.14 = (f32[2,256,768]{2,1,0:T(8,128)S(1)}, f32[2,256,768]{2,1,0:T(8,128)}, u32[]{:S(2)}) copy-start(f32[2,256,768]{2,1,0:T(8,128)} %copy-done.13) | copy-start | bytes 4718596
  632.5 114.6 %copy-start.23 = (f32[2,256,768]{2,1,0:T(8,128)S(1)}, f32[2,256,768]{2,1,0:T(8,128)}, u32[]{:S(2)}) copy-start(f32[2,256,768]{2,1,0:T(8,128)} %get-tuple-element.364) | copy-start | bytes 4718596
  (64 other events, 241.4 us)
Sparse Core Ops, SparseCore 0:
  16.6 12.5 all-gather.8
  53.9 9.2 reduce-scatter.8
  68.2 11.0 all-gather.10
  105.0 9.3 reduce-scatter.10
  143.0 14.0 all-gather.12
  181.0 10.2 reduce-scatter.12
  194.8 11.0 all-gather.14
  208.1 10.9 all-gather.16
  236.5 46.2 reduce-scatter.16
  284.9 10.3 reduce-scatter.14
  301.4 11.0 all-gather.18
  326.8 86.5 reduce-scatter.18
  444.6 10.0 all-gather.20
  500.0 9.3 reduce-scatter.20
  516.6 11.0 all-gather.22
  577.0 9.3 reduce-scatter.22
  594.9 437.7 all-reduce.5
where the time goes:
time: 1060 us; the launch traced here: 1050 us
  waiting for transfers between devices  558 us (53%)
  local copies, waits for them, and re-layouts  153 us (14%)
  matrix products  134 us (13%)
  other arithmetic  111 us (10%)
  blocking collectives  67.1 us (6%)
  between operations  15.6 us (1%)
    psum x1, waiting for transfers between devices, shards(): matrices = lax.psum(matrices, 'dp')  281 us
    reduce_scatter x4, waiting for transfers between devices, backward_pass(): lax.psum_scatter(partial_out.astype(jnp.bfloat16), 'head', scatter_dimens...  136 us
    scatter x1, local copies, waits for them, and re-layouts, spread_rows(): jnp.zeros((npatch, model_width), jnp.float32).at[positions].set(values)  69.6 us
    psum x1, blocking collectives, shards(): lax.psum((both_slots(vectors[0]), both_slots(vectors[1]), both_slots(vect...  43.1 us
    ppermute x2, waiting for transfers between devices, passed_along(): return lax.ppermute(block, axis, route)  31.5 us
    all_gather x2, waiting for transfers between devices, forward_pass(): lax.all_gather(normed.astype(jnp.bfloat16), 'head', axis=0, tiled=True)  26.5 us
    unnamed x149, local copies, waits for them, and re-layouts  26 us
    dot_general x2, matrix products, mlp_front(): jnp.einsum('iqd,df->iqf', normed_two, up_weight, preferred_element_type=j...  25.8 us
  transfers between devices with their start and end apart: 19, of which 16 were waited for; matrix products, arithmetic and copies ran while one was open for 14% of the time, Pallas kernels for 0%

commit v1 on v0

v1 whole, which is shorter than its diff:
```python
import functools
import math

import jax
import jax.numpy as jnp
from jax import lax
from jax.experimental import pallas as pl
from jax.experimental.pallas import tpu as pltpu
from jax.sharding import PartitionSpec as P

HEADS = 12
EPSILON = 1e-06
BF = jnp.bfloat16
F32 = jnp.float32
ROWS_AT_ONCE = 64
NN = ((1,), (0,))
NT = ((1,), (1,))
TN = ((0,), (0,))
SWAP = ((0, 1), (1, 0))
VMEM_BYTES = 60 * 1024 * 1024


def dot(left, right, dims=NN):
    return lax.dot_general(left, right, (dims, ((), ())), preferred_element_type=F32)


def row_loop(rows, body):
    def step(index, carry):
        body(pl.ds(pl.multiple_of(index * ROWS_AT_ONCE, ROWS_AT_ONCE), ROWS_AT_ONCE))
        return carry

    lax.fori_loop(0, rows // ROWS_AT_ONCE, step, 0)


def standardize(values):
    centred = values - jnp.mean(values, -1, keepdims=True)
    inv_std = lax.rsqrt(jnp.mean(centred * centred, -1, keepdims=True) + EPSILON)
    return centred * inv_std, inv_std


def norm_into(source, target, gain, bias):
    def body(rows):
        scaled, _ = standardize(source[rows, :])
        target[rows, :] = (scaled * gain + bias).astype(BF)

    row_loop(source.shape[0], body)


def fold_rows(values):
    return jnp.sum(values.reshape(-1, 8, values.shape[-1]), 0)


def norm_back(grad, scaled, inv_std, gain):
    scaled_grad = grad * gain
    return inv_std * (
        scaled_grad
        - jnp.mean(scaled_grad, -1, keepdims=True)
        - scaled * jnp.mean(scaled_grad * scaled, -1, keepdims=True)
    )


class Weights:
    NAMES = ("qkv", "out", "up", "down")

    def __init__(self, sources, buffers, sems, names=NAMES):
        self.buffers = dict(zip(self.NAMES, buffers))
        self.copies = {}
        for at, name in enumerate(self.NAMES):
            if name not in names:
                continue
            for half in range(2):
                self.copies[name, half] = pltpu.make_async_copy(
                    sources[2 * at + half], self.buffers[name].at[half], sems.at[at, half]
                )

    def start(self, order):
        for name in order:
            for half in range(2):
                self.copies[name, half].start()

    def wait(self, name):
        for half in range(2):
            self.copies[name, half].wait()

    def __getitem__(self, name):
        return self.buffers[name]


def weight_scratch(width, local, hidden):
    return [
        pltpu.VMEM((2, 3, width, local), BF),
        pltpu.VMEM((2, local, width), BF),
        pltpu.VMEM((2, width, hidden), BF),
        pltpu.VMEM((2, hidden, width), BF),
        pltpu.SemaphoreType.DMA((4, 2)),
    ]


def head_masks():
    lanes = lax.broadcasted_iota(jnp.int32, (1, 128), 1)
    low = (lanes < 64).astype(F32)
    return low.astype(BF), (1.0 - low).astype(BF)


def forward(rows_all, ctx, vec, up_bias, weights, keep, result_fn):
    width = rows_all.shape[1]
    row_count = rows_all.shape[0] - ctx
    normed, queries, keys, values, probs, mixed = (
        keep[name] for name in ("N", "Q", "K", "V", "P", "O")
    )
    norm_into(rows_all, normed, vec[0:1, :], vec[2:3, :])
    weights.wait("qkv")
    local = weights["qkv"].shape[3]
    for half in range(2):
        cols = slice(half * local, (half + 1) * local)
        queries[:, cols] = (dot(normed[ctx:, :], weights["qkv"][half, 0]) * 0.125).astype(BF)
        keys[:, cols] = dot(normed[...], weights["qkv"][half, 1]).astype(BF)
        values[:, cols] = dot(normed[...], weights["qkv"][half, 2]).astype(BF)
    masks = head_masks()

    def attend(pair, carry):
        cols = pl.ds(pl.multiple_of(pair * 128, 128), 128)
        query, key = queries[:, cols], keys[:, cols]
        value_t = values[:, cols].T
        outs = []
        for at in range(2):
            scores = dot(key, query * masks[at], NT)
            weight = jnp.exp(scores - jnp.max(scores, 0, keepdims=True))
            prob = (weight * (1.0 / jnp.sum(weight, 0, keepdims=True))).astype(BF)
            probs[2 * pair + at] = prob
            outs.append(dot(value_t[64 * at : 64 * at + 64], prob))
        mixed[:, cols] = jnp.concatenate(outs, 0).T.astype(BF)
        return carry

    lax.fori_loop(0, HEADS // 2, attend, 0)
    weights.wait("out")
    attended = dot(mixed[:, :local], weights["out"][0]) + dot(mixed[:, local:], weights["out"][1])
    hidden, normed_two = keep["H"], keep["M"]
    keep["A"][...] = attended.astype(keep["A"].dtype)
    hidden[...] = rows_all[ctx:, :] + vec[4:5, :] * attended
    norm_into(hidden, normed_two, vec[1:2, :], vec[3:4, :])
    weights.wait("up")
    weights.wait("down")
    fed = keep["F"]
    fed[...] = jnp.broadcast_to(vec[6:7, :], fed.shape)
    step = 512
    per_half = weights["up"].shape[2] // step
    for half in range(2):

        def feed(chunk, carry):
            cols = pl.ds(pl.multiple_of(chunk * step, step), step)
            pre = dot(normed_two[...], weights["up"][half, :, cols]) + up_bias[half, :, cols]
            phi = 0.5 + 0.5 * lax.erf(pre * math.sqrt(0.5))
            act = (pre * phi).astype(BF)
            if "G" in keep:
                keep["G"][half, :, cols] = act
                density = jnp.exp(pre * pre * -0.5) * (1.0 / math.sqrt(2.0 * math.pi))
                keep["D"][half, :, cols] = (phi + pre * density).astype(BF)
            fed[...] += dot(act, weights["down"][half, cols, :])
            return carry

        lax.fori_loop(0, per_half, feed, 0)

    def finish(rows):
        result_fn(rows, hidden[rows, :] + vec[5:6, :] * fed[rows, :])

    row_loop(row_count, finish)


def backward(rows_all, ctx, out_grad_fn, vec, weights, keep, grads, work, sums, up_bias_grad):
    width = rows_all.shape[1]
    row_count = rows_all.shape[0] - ctx
    local = width // 2
    grad_in = work["dH"]
    for at in range(8):
        sums[at] = jnp.zeros((8, width), F32)

    def enter(rows):
        grad = out_grad_fn(rows)
        grad_in[rows, :] = grad
        branch = vec[5:6, :] * grad
        sums[5] += fold_rows(grad * keep["F"][rows, :].astype(F32))
        sums[6] += fold_rows(branch)
        grads["dF"][rows, :] = branch.astype(BF)

    row_loop(row_count, enter)
    weights.wait("down")
    weights.wait("up")
    grad_mid = work["dM"]
    grad_mid[...] = jnp.zeros_like(grad_mid)
    step = 512
    per_half = weights["up"].shape[2] // step
    for half in range(2):

        def feed(chunk, carry):
            cols = pl.ds(pl.multiple_of(chunk * step, step), step)
            act_grad = dot(grads["dF"][...], weights["down"][half, cols, :], NT)
            pre_grad = act_grad * keep["D"][half, :, cols].astype(F32)
            up_bias_grad[half, :, cols] = jnp.sum(pre_grad, 0, keepdims=True)
            pre_grad = pre_grad.astype(BF)
            grads["dU"][half, :, cols] = pre_grad
            grad_mid[...] += dot(pre_grad, weights["up"][half, :, cols], NT)
            return carry

        lax.fori_loop(0, per_half, feed, 0)

    def middle(rows):
        scaled, inv_std = standardize(keep["H"][rows, :])
        grad = grad_mid[rows, :]
        sums[1] += fold_rows(grad * scaled)
        sums[3] += fold_rows(grad)
        hidden_grad = grad_in[rows, :] + norm_back(grad, scaled, inv_std, vec[1:2, :])
        grad_in[rows, :] = hidden_grad
        sums[4] += fold_rows(hidden_grad * keep["A"][rows, :].astype(F32))
        grads["dA"][rows, :] = (vec[4:5, :] * hidden_grad).astype(BF)

    row_loop(row_count, middle)
    weights.wait("out")
    mix_grad = work["dO"]
    for half in range(2):
        mix_grad[:, half * local : (half + 1) * local] = dot(
            grads["dA"][...], weights["out"][half], NT
        ).astype(BF)
    masks = head_masks()

    def attend(pair, carry):
        cols = pl.ds(pl.multiple_of(pair * 128, 128), 128)
        query, key, value = keep["Q"][:, cols], keep["K"][:, cols], keep["V"][:, cols]
        out_grad = mix_grad[:, cols]
        key_t = key.T
        value_grad = key_grad = None
        query_grads = []
        for at in range(2):
            prob = keep["P"][2 * pair + at]
            own_grad = out_grad * masks[at]
            part = dot(prob, own_grad)
            value_grad = part if value_grad is None else value_grad + part
            prob_grad = dot(value, own_grad, NT)
            wide = prob.astype(F32)
            product = wide * prob_grad
            score_grad = (product - wide * jnp.sum(product, 0, keepdims=True)).astype(BF)
            part = dot(score_grad, query * masks[at])
            key_grad = part if key_grad is None else key_grad + part
            query_grads.append(dot(key_t[64 * at : 64 * at + 64], score_grad))
        grads["dV"][:, cols] = value_grad.astype(BF)
        grads["dK"][:, cols] = key_grad.astype(BF)
        grads["dQ"][:, cols] = (jnp.concatenate(query_grads, 0).T * 0.125).astype(BF)
        return carry

    lax.fori_loop(0, HEADS // 2, attend, 0)
    weights.wait("qkv")
    grad_all = work["dN"]
    qkv = weights["qkv"]
    for half in range(2):
        cols = slice(half * local, (half + 1) * local)
        part = dot(grads["dK"][:, cols], qkv[half, 1], NT) + dot(
            grads["dV"][:, cols], qkv[half, 2], NT
        )
        if half == 0:
            grad_all[...] = part
        else:
            grad_all[...] += part
        grad_all[ctx:, :] += dot(grads["dQ"][:, cols], qkv[half, 0], NT)

    def leave(rows):
        scaled, inv_std = standardize(rows_all[rows, :])
        grad = grad_all[rows, :]
        sums[0] += fold_rows(grad * scaled)
        sums[2] += fold_rows(grad)
        grad_all[rows, :] = norm_back(grad, scaled, inv_std, vec[0:1, :])

    row_loop(rows_all.shape[0], leave)


def write_sums(sums, target):
    for at in range(8):
        target[at : at + 1, :] = jnp.sum(sums[at], 0, keepdims=True)


def pick_rows(order_column, patches):
    places = lax.broadcasted_iota(jnp.int32, (order_column.shape[0], patches.shape[0]), 1)
    return dot((places == order_column).astype(F32).astype(BF), patches)


KEPT = ("X", "N", "Q", "K", "V", "P", "O", "A", "H", "M", "G", "D", "F")
GRADS = ("dF", "dU", "dA", "dQ", "dK", "dV")
OPERANDS = ("dF", "G", "dU", "M", "dA", "O", "dQ", "dK", "dV", "N")


def kept_shapes(rows, keys, width, hidden):
    return {
        "X": ((rows, width), BF),
        "N": ((keys, width), BF),
        "Q": ((rows, width), BF),
        "K": ((keys, width), BF),
        "V": ((keys, width), BF),
        "P": ((HEADS, keys, rows), BF),
        "O": ((rows, width), BF),
        "A": ((rows, width), BF),
        "H": ((rows, width), F32),
        "M": ((rows, width), BF),
        "G": ((2, rows, hidden), BF),
        "D": ((2, rows, hidden), BF),
        "F": ((rows, width), F32),
    }


def grad_shapes(rows, keys, width, hidden):
    return {
        "dF": ((rows, width), BF),
        "dU": ((2, rows, hidden), BF),
        "dA": ((rows, width), BF),
        "dQ": ((rows, width), BF),
        "dK": ((keys, width), BF),
        "dV": ((keys, width), BF),
    }


def vmem(shape_type):
    return pltpu.VMEM(*shape_type)


ONCE = pl.Buffered(1)


def whole(shape):
    return pl.BlockSpec(tuple(shape), lambda _: (0,) * len(shape), pipeline_mode=ONCE)


def image_of(array, image):
    return pl.BlockSpec(
        (None,) + array.shape[1:],
        lambda _: (image,) + (0,) * (array.ndim - 1),
        pipeline_mode=ONCE,
    )


ANY = pl.BlockSpec(memory_space=pl.ANY)


def shape_of(shape_type):
    return jax.ShapeDtypeStruct(*shape_type)


def nothing(shapes):
    return pl.pallas_call(
        lambda *refs: None,
        out_shape=[shape_of(s) for s in shapes],
        out_specs=[ANY] * len(shapes),
        name="no_values",
    )()


def params_of(**extra):
    return pltpu.CompilerParams(vmem_limit_bytes=VMEM_BYTES, **extra)


def block_cost(rows, keys, width, hidden, passes):
    flops = 2 * rows * width * (2 * width + 4 * hidden) + 4 * keys * width * width
    flops += 4 * rows * keys * width
    return pl.CostEstimate(flops=passes * flops, bytes_accessed=24_000_000, transcendentals=0)


def encoder_forward(image, which, patches, order_column, vec, up_bias, matrices, save):
    _, places, width = patches.shape
    rows = places // 2
    hidden = matrices[4].shape[1]
    local = width // 2
    shapes = kept_shapes(rows, rows, width, hidden)
    names = [n for n in KEPT]

    def kernel(patch_ref, order_ref, vec_ref, bias_ref, *refs):
        sources, refs = refs[:8], refs[8:]
        result, refs = refs[0], refs[1:]
        if save:
            keep = dict(zip(names, refs[: len(names)]))
            refs = refs[len(names) :]
        else:
            own = [n for n in names if n not in ("X", "G", "D")]
            keep = dict(zip(own, refs[: len(own)]))
            refs = refs[len(own) :]
        rows_ref, refs = refs[0], refs[1:]
        weights = Weights(sources, refs[:4], refs[4])
        weights.start(("qkv", "out", "up", "down"))
        rows_ref[...] = pick_rows(order_ref[...], patch_ref[...])
        if save:
            keep["X"][...] = rows_ref[...].astype(BF)

        def result_fn(rows_at, value):
            result[rows_at, :] = value.astype(BF)

        forward(rows_ref, 0, vec_ref, bias_ref, weights, keep, result_fn)

    out_shapes = [((rows, width), BF)] + ([shapes[n] for n in names] if save else [])
    scratch = [] if save else [vmem(shapes[n]) for n in names if n not in ("X", "G", "D")]
    scratch = scratch + [pltpu.VMEM((rows, width), F32)] + weight_scratch(width, local, hidden)
    order_spec = pl.BlockSpec(
        (None, rows, 1), lambda _: (image, which, 0), pipeline_mode=ONCE
    )
    return pl.pallas_call(
        kernel,
        grid=(1,),
        out_shape=[shape_of(s) for s in out_shapes],
        in_specs=[image_of(patches, image), order_spec, whole(vec.shape), whole(up_bias.shape)]
        + [ANY] * 8,
        out_specs=[whole(s[0]) for s in out_shapes],
        scratch_shapes=scratch,
        compiler_params=params_of(),
        cost_estimate=block_cost(rows, rows, width, hidden, 1),
        name="encoder_forward" if save else "encoder_targets",
    )(patches, order_column, vec, up_bias, *matrices)


def encoder_backward(image, latent_grad, cotangent, order_row, kept, vec, matrices):
    rows, width = latent_grad.shape
    hidden = matrices[4].shape[1]
    local = width // 2
    shapes = grad_shapes(rows, rows, width, hidden)
    names = list(GRADS)

    def kernel(back_ref, cot_ref, order_ref, vec_ref, *refs):
        sources, refs = refs[:8], refs[8:]
        keep = dict(zip(KEPT, refs[: len(KEPT)]))
        refs = refs[len(KEPT) :]
        input_grad, vec_grad, bias_grad, refs = refs[0], refs[1], refs[2], refs[3:]
        grads = dict(zip(names, refs[: len(names)]))
        refs = refs[len(names) :]
        rows_ref, d_hidden, d_mid, d_out, d_norm, sums = refs[:6]
        weights = Weights(sources, refs[6:10], refs[10])
        weights.start(("down", "up", "out", "qkv"))
        work = {"dH": d_hidden, "dM": d_mid, "dO": d_out, "dN": d_norm}
        rows_ref[...] = keep["X"][...].astype(F32)

        def out_grad_fn(rows_at):
            return cot_ref[rows_at, :].astype(F32) + back_ref[rows_at, :].astype(F32)

        backward(rows_ref, 0, out_grad_fn, vec_ref, weights, keep, grads, work, sums, bias_grad)
        write_sums(sums, vec_grad)

        def join(rows_at):
            total = d_norm[rows_at, :] + d_hidden[rows_at, :]
            high = total.astype(BF)
            d_out[rows_at, :] = high
            grads_low[rows_at, :] = (total - high.astype(F32)).astype(BF)

        grads_low = refs[11]
        row_loop(rows, join)

        def place(index, carry):
            first = pl.multiple_of(index * 128, 128)
            places = lax.broadcasted_iota(jnp.int32, (128, rows), 0) + first
            hot = (places == order_ref[...]).astype(F32).astype(BF)
            input_grad[pl.ds(first, 128), :] = dot(hot, d_out[...]) + dot(hot, grads_low[...])
            return carry

        lax.fori_loop(0, input_grad.shape[0] // 128, place, 0)

    out_shapes = [((2 * rows, width), F32), ((8, width), F32), ((2, 1, hidden), F32)]
    out_shapes += [shapes[n] for n in names]
    scratch = [
        pltpu.VMEM((rows, width), F32),
        pltpu.VMEM((rows, width), F32),
        pltpu.VMEM((rows, width), F32),
        pltpu.VMEM((rows, width), BF),
        pltpu.VMEM((rows, width), F32),
        pltpu.VMEM((8, 8, width), F32),
    ]
    scratch += weight_scratch(width, local, hidden) + [pltpu.VMEM((rows, width), BF)]
    order_spec = pl.BlockSpec((None, 1, rows), lambda _: (image, 0, 0), pipeline_mode=ONCE)
    outs = pl.pallas_call(
        kernel,
        grid=(1,),
        out_shape=[shape_of(s) for s in out_shapes],
        in_specs=[whole(latent_grad.shape), image_of(cotangent, image), order_spec, whole(vec.shape)]
        + [ANY] * 8
        + [whole(k.shape) for k in kept],
        out_specs=[whole(s[0]) for s in out_shapes],
        scratch_shapes=scratch,
        compiler_params=params_of(),
        cost_estimate=block_cost(rows, rows, width, hidden, 1),
        name="encoder_backward",
    )(latent_grad, cotangent, order_row, vec, *matrices, *kept)
    grads = dict(zip(names, outs[3:]))
    grads.update(dict(zip(KEPT, kept)))
    return outs[0], outs[1], outs[2], [grads[n] for n in OPERANDS]


def operand_shapes(rows, keys, width, hidden):
    shapes = dict(grad_shapes(rows, keys, width, hidden))
    shapes.update(kept_shapes(rows, keys, width, hidden))
    return [shapes[n] for n in OPERANDS]


def regressor_block(image, latent, codes, token, cotangent, vec, up_bias, matrices):
    ctx, width = latent.shape
    rows = codes.shape[1] - ctx
    keys = rows + ctx
    hidden = matrices[4].shape[1]
    local = width // 2
    kept = kept_shapes(rows, keys, width, hidden)
    shapes = grad_shapes(rows, keys, width, hidden)
    own = [n for n in KEPT if n != "X" and n not in OPERANDS]

    def kernel(latent_ref, code_ref, token_ref, cot_ref, vec_ref, bias_ref, *refs):
        sources, refs = refs[:8], refs[8:]
        result, back, input_grad, vec_grad, bias_grad = refs[:5]
        refs = refs[5:]
        named = dict(zip(OPERANDS, refs[: len(OPERANDS)]))
        refs = refs[len(OPERANDS) :]
        keep = dict(named)
        keep.update(zip(own, refs[: len(own)]))
        refs = refs[len(own) :]
        rows_ref, d_hidden, d_mid, d_out, sums = refs[:5]
        weights = Weights(sources, refs[5:9], refs[9])
        weights.start(("qkv", "out", "up", "down"))

        def fill(rows_at):
            rows_ref[rows_at, :] = latent_ref[rows_at, :].astype(F32) + code_ref[rows_at, :]
            lower = pl.ds(rows_at.start + ctx, ROWS_AT_ONCE)
            rows_ref[lower, :] = token_ref[...] + code_ref[lower, :]

        row_loop(ctx, fill)

        def result_fn(rows_at, value):
            result[rows_at, :] = value.astype(BF)

        forward(rows_ref, ctx, vec_ref, bias_ref, weights, keep, result_fn)
        work = {"dH": d_hidden, "dM": d_mid, "dO": d_out, "dN": input_grad}

        def out_grad_fn(rows_at):
            return cot_ref[rows_at, :].astype(F32)

        weights.wait = lambda name: None
        backward(
            rows_ref, ctx, out_grad_fn, vec_ref, weights, keep, named, work, sums, bias_grad
        )

        def leave(rows_at):
            back[rows_at, :] = input_grad[rows_at, :].astype(BF)
            lower = pl.ds(rows_at.start + ctx, ROWS_AT_ONCE)
            total = input_grad[lower, :] + d_hidden[rows_at, :]
            input_grad[lower, :] = total
            sums[7] += fold_rows(total)

        row_loop(rows, leave)
        write_sums(sums, vec_grad)

    out_shapes = [
        ((rows, width), BF),
        ((ctx, width), BF),
        ((keys, width), F32),
        ((8, width), F32),
        ((2, 1, hidden), F32),
    ] + operand_shapes(rows, keys, width, hidden)
    scratch = [vmem(kept[n]) for n in own]
    scratch += [
        pltpu.VMEM((keys, width), F32),
        pltpu.VMEM((rows, width), F32),
        pltpu.VMEM((rows, width), F32),
        pltpu.VMEM((rows, width), BF),
        pltpu.VMEM((8, 8, width), F32),
    ]
    scratch += weight_scratch(width, local, hidden)
    outs = pl.pallas_call(
        kernel,
        grid=(1,),
        out_shape=[shape_of(s) for s in out_shapes],
        in_specs=[
            whole(latent.shape),
            image_of(codes, image),
            whole(token.shape),
            image_of(cotangent, image),
            whole(vec.shape),
            whole(up_bias.shape),
        ]
        + [ANY] * 8,
        out_specs=[whole(s[0]) for s in out_shapes],
        scratch_shapes=scratch,
        compiler_params=params_of(),
        cost_estimate=block_cost(rows, keys, width, hidden, 2),
        name="regressor_block",
    )(latent, codes, token, cotangent, vec, up_bias, *matrices)
    return outs


def weight_grad(name, lefts, rights, first_rows, split_left, step, halves):
    images = len(lefts)
    wide = (lefts if split_left else rights)[0]
    other = (rights if split_left else lefts)[0]
    if wide.ndim == 3:
        blocks = (wide.shape[0], wide.shape[2] // step)
        wide_spec = pl.BlockSpec((None, wide.shape[1], step), lambda h, c: (h, 0, c))
        width = wide.shape[2]
    else:
        blocks = (halves, wide.shape[1] // halves // step)
        wide_spec = pl.BlockSpec(
            (wide.shape[0], step), lambda h, c: (0, h * blocks[1] + c)
        )
        width = wide.shape[1] // halves
    other_spec = pl.BlockSpec(other.shape, lambda h, c: (0, 0))
    if split_left:
        out = ((halves, width, other.shape[1]), BF)
        out_spec = pl.BlockSpec((None, step, other.shape[1]), lambda h, c: (h, c, 0))
    else:
        out = ((halves, other.shape[1], width), BF)
        out_spec = pl.BlockSpec((None, other.shape[1], step), lambda h, c: (h, 0, c))

    def kernel(*refs):
        total = None
        for at in range(images):
            left, right = refs[at][...], refs[images + at][...]
            if first_rows:
                left = left[first_rows:]
            part = dot(left, right, TN)
            total = part if total is None else total + part
        refs[-1][...] = total.astype(BF)

    specs = ([wide_spec] * images + [other_spec] * images) if split_left else (
        [other_spec] * images + [wide_spec] * images
    )
    rows = rights[0].shape[-2]
    return pl.pallas_call(
        kernel,
        grid=blocks,
        out_shape=shape_of(out),
        in_specs=specs,
        out_specs=out_spec,
        compiler_params=params_of(),
        cost_estimate=pl.CostEstimate(
            flops=2 * images * rows * halves * width * other.shape[1],
            bytes_accessed=8_000_000,
            transcendentals=0,
        ),
        name=name,
    )(*lefts, *rights)


def matrix_grads(operands, ctx):
    named = [dict(zip(OPERANDS, one)) for one in operands]

    def column(name):
        return [one[name] for one in named]

    down = weight_grad("down_grad", column("G"), column("dF"), 0, True, 512, 2)
    up = weight_grad("up_grad", column("M"), column("dU"), 0, False, 512, 2)
    out = weight_grad("out_grad", column("O"), column("dA"), 0, True, 384, 2)
    query = weight_grad("query_grad", column("N"), column("dQ"), ctx, False, 384, 2)
    key = weight_grad("key_grad", column("N"), column("dK"), 0, False, 384, 2)
    value = weight_grad("value_grad", column("N"), column("dV"), 0, False, 384, 2)
    return down, up, out, query, key, value


def place_code(positions, model_width):
    half_width = model_width // 2
    frequency = jnp.exp(
        jnp.arange(half_width, dtype=F32) * (-math.log(10000.0) / half_width)
    )
    angles = positions.astype(F32)[..., None] * frequency
    return jnp.concatenate([jnp.sin(angles), jnp.cos(angles)], -1)


def shards(
    patches,
    order,
    cotangent,
    norm_gains,
    norm_biases,
    layer_scales,
    qkv_weight,
    out_weight,
    up_weight,
    up_bias,
    down_weight,
    down_bias,
    mask_token,
):
    images, places, width = patches.shape
    rows = places // 2
    hidden = up_weight.shape[2]
    local = width // 2
    encoder = lax.axis_index("stream") == 0

    def swapped(value):
        return lax.ppermute(value, "head", SWAP)

    own = (qkv_weight[0], out_weight[0], up_weight[0], down_weight[0])
    matrices = []
    for value in own:
        matrices += [value, swapped(value)]
    bias_pair = jnp.stack([up_bias[0], swapped(up_bias[0])]).astype(F32)[:, None, :]
    vec = jnp.concatenate(
        [
            norm_gains[0],
            norm_biases[0],
            layer_scales[0],
            down_bias[0][None],
            jnp.zeros((1, width), F32),
        ]
    )
    token = mask_token[None]
    cotangent = cotangent[0]
    order_column = order[:, :, None]
    order_row = order[:, None, :]

    kept_list = list(kept_shapes(rows, rows, width, hidden).values())
    row_shape = ((rows, width), BF)
    code_shape = ((images, places, width), F32)
    operand_list = [
        operand_shapes(rows, rows, width, hidden),
        operand_shapes(rows, places, width, hidden),
    ]

    kept, latents = [], []
    codes = None
    for image in range(images):

        def run_encoder():
            outs = encoder_forward(
                image, 0, patches, order_column, vec, up_bias=bias_pair, matrices=matrices, save=True
            )
            return tuple(outs) + ((nothing([code_shape])[0],) if image == 0 else ())

        def run_other():
            outs = nothing([row_shape] + kept_list)
            return tuple(outs) + ((place_code(order, width),) if image == 0 else ())

        outs = lax.cond(encoder, run_encoder, run_other)
        if image == 0:
            codes = outs[-1]
            outs = outs[:-1]
        latents.append(outs[0])
        kept.append(outs[1:])
    arrived = [lax.ppermute(one, "stream", [(0, 1)]) for one in latents]

    features, returned, reg_inputs, reg_vecs, reg_biases, reg_operands = [], [], [], [], [], []
    for image in range(images):

        def run_targets():
            (target,) = encoder_forward(
                image, 1, patches, order_column, vec, bias_pair, matrices, save=False
            )
            rest = nothing(
                [row_shape, ((places, width), F32), ((8, width), F32), ((2, 1, hidden), F32)]
                + operand_list[1]
            )
            return (target,) + tuple(rest)

        def run_regressor():
            return tuple(
                regressor_block(
                    image, arrived[image], codes, token, cotangent, vec, bias_pair, matrices
                )
            )

        outs = lax.cond(encoder, run_targets, run_regressor)
        features.append(outs[0])
        returned.append(lax.ppermute(outs[1], "stream", [(1, 0)]))
        reg_inputs.append(outs[2])
        reg_vecs.append(outs[3])
        reg_biases.append(outs[4])
        reg_operands.append(outs[5:])

    input_grads, vec_grads, bias_grads, enc_operands = [], [], [], []
    for image in range(images):

        def run_backward():
            got = encoder_backward(
                image, returned[image], cotangent, order_row[:, :, :rows], kept[image], vec, matrices
            )
            return (got[0], got[1], got[2]) + tuple(got[3])

        def run_pass():
            return (reg_inputs[image], reg_vecs[image], reg_biases[image]) + tuple(
                nothing(operand_list[0])
            )

        outs = lax.cond(encoder, run_backward, run_pass)
        input_grads.append(outs[0])
        vec_grads.append(outs[1])
        bias_grads.append(outs[2])
        enc_operands.append(outs[3:])

    parts = lax.cond(
        encoder,
        lambda: matrix_grads(enc_operands, 0),
        lambda: matrix_grads(reg_operands, rows),
    )
    vec_grad = sum(vec_grads)
    bias_grad = sum(bias_grads)[:, 0]

    def reduced(value, dim):
        mine = value[0].astype(F32) + swapped(value[1]).astype(F32)
        part = lax.psum_scatter(mine.astype(BF), "dp", scatter_dimension=dim, tiled=True)
        return lax.all_gather(part, "dp", axis=dim, tiled=True).astype(F32)

    down, up, out, query, key, value = (reduced(one, 0) for one in parts)
    bias_own = bias_grad[0] + swapped(bias_grad[1])
    bias_total = lax.psum(bias_own, "dp")
    totals = lax.psum(vec_grad, ("dp", "head"))
    token_grad = lax.psum(jnp.where(encoder, 0.0, totals[7]), "stream")

    latent_out = jnp.where(encoder, jnp.stack(latents), jnp.stack(arrived))
    return (
        latent_out,
        jnp.stack(features)[None],
        jnp.stack(input_grads)[None],
        totals[0:2][None],
        totals[2:4][None],
        totals[4:6][None],
        jnp.stack([query, key, value])[None],
        out[None],
        up[None],
        bias_total[None],
        down[None],
        totals[6][None],
        token_grad,
    )


def solution(mesh):
    in_specs = (
        P(("dp", "head"), None, None),
        P(("dp", "head"), None),
        P("stream", ("dp", "head"), None, None),
        P("stream", None, None),
        P("stream", None, None),
        P("stream", None, None),
        P("stream", None, None, "head"),
        P("stream", "head", None),
        P("stream", None, "head"),
        P("stream", "head"),
        P("stream", "head", None),
        P("stream", None),
        P(),
    )
    out_specs = (
        P(("dp", "head"), None, None),
        P("stream", ("dp", "head"), None, None),
        P("stream", ("dp", "head"), None, None),
        P("stream", None, None),
        P("stream", None, None),
        P("stream", None, None),
        P("stream", None, None, "head"),
        P("stream", "head", None),
        P("stream", None, "head"),
        P("stream", "head"),
        P("stream", "head", None),
        P("stream", None),
        P(),
    )
    return jax.shard_map(shards, mesh=mesh, in_specs=in_specs, out_specs=out_specs, check_vma=False)
```

time: 1060 us -> 740 us (0.70)
  waiting for transfers between devices: 558 us -> 304 us
  Pallas kernels: 0 us -> 146 us
  blocking collectives: 67.1 us -> 213 us
  local copies, waits for them, and re-layouts: 153 us -> 11.3 us
  matrix products: 134 us -> 0 us
  other arithmetic: 111 us -> 31.5 us
    psum x1 -> x0, waiting for transfers between devices: 281 us -> none  [shards(): matrices = lax.psum(matrices, 'dp')]
    pallas_call x0 -> x15, Pallas kernels: none -> 146 us  [the longest x4 72.3 us: encoder_forward(): pl.pallas_call(kernel, grid=(1,), out_shape=[shape_of(s) for s in out_sha...]
    dot_general x29 -> x0, matrix products: 134 us -> none  [the longest x2 25.8 us: mlp_front(): jnp.einsum('iqd,df->iqf', normed_two, up_weight, preferred_element_type=j...]
    all_gather x0 -> x4, blocking collectives: none -> 129 us  [reduced(): return lax.all_gather(part, 'dp', axis=dim, tiled=True).astype(F32)]
    scatter x1 -> x0, local copies, waits for them, and re-layouts: 69.6 us -> none  [spread_rows(): jnp.zeros((npatch, model_width), jnp.float32).at[positions].set(values)]
    reduce_sum x18 -> x0, other arithmetic: 33.7 us -> none  [the longest x4 10.5 us: norm_back(): jnp.sum(gradient * scaled, (0, 1))]
    unnamed x149 -> x24, local copies, waits for them, and re-layouts: 26 us -> 0.79 us
    reduce_scatter x8 -> x6, waiting for transfers between devices: 164 us -> 189 us  [reduced(): lax.psum_scatter(mine.astype(BF), 'dp', scatter_dimension=dim, tiled=True)]
  transfers between devices with their start and end apart: 19 -> 24, of which waited for: 16 -> 16; matrix products, arithmetic and copies ran while one was open for 14% -> 4% of each run, Pallas kernels for 0% -> 11%
where the time goes in v1:
time: 740 us; the launch traced here: 731 us
  waiting for transfers between devices  304 us (41%)
  blocking collectives  213 us (29%)
  Pallas kernels  146 us (20%)
  other arithmetic  31.5 us (4%)
  between operations  14.7 us (2%)
  local copies, waits for them, and re-layouts  11.3 us (2%)
  starting transfers between devices  9.82 us (1%)
    reduce_scatter x6, waiting for transfers between devices, reduced(): lax.psum_scatter(mine.astype(BF), 'dp', scatter_dimension=dim, tiled=True)  189 us
    all_gather x4, blocking collectives, reduced(): return lax.all_gather(part, 'dp', axis=dim, tiled=True).astype(F32)  129 us
    pallas_call x4, Pallas kernels, encoder_forward(): pl.pallas_call(kernel, grid=(1,), out_shape=[shape_of(s) for s in out_sha...  72.3 us
    all_gather x2, waiting for transfers between devices, reduced(): return lax.all_gather(part, 'dp', axis=dim, tiled=True).astype(F32)  69.3 us
    psum x1, blocking collectives, shards(): totals = lax.psum(vec_grad, ('dp', 'head'))  59.9 us
    pallas_call x2, Pallas kernels, encoder_backward(): pl.pallas_call(kernel, grid=(1,), out_shape=[shape_of(s) for s in out_sha...  48.7 us
    pallas_call x6, Pallas kernels, weight_grad(): pl.pallas_call(kernel, grid=blocks, out_shape=shape_of(out), in_specs=spe...  25.2 us
    ppermute x12, waiting for transfers between devices, swapped(): return lax.ppermute(value, 'head', SWAP)  24 us
  transfers between devices with their start and end apart: 24, of which 16 were waited for; matrix products, arithmetic and copies ran while one was open for 4% of the time, Pallas kernels for 11%

profile of v1, /device:TPU:0, one launch (start us, length us, event | category | flops | bytes accessed | tf_op | source)
XLA Modules:
  0.0 730.9 jit_solution(6992172941494483466)
XLA Ops:
  11.3 7.6 %collective-permute-done = bf16[1536]{0:T(1024)(128)(2,1)S(1)} collective-permute-done((bf16[1536]{0:T(1024)(128)(2,1)S(1)}, bf16[1536]{0:T(1024)(128)(2,1)S(1)}, u32[]{:S(2)}, u32[]{:S(2)}) %collective-permute-start) | collective-permute-done | bytes 3104 | tf_op jit(solution)/shard_map/ppermute | solution.py:684
  19.7 19.8 %conditional.7 = (bf16[256,768]{1,0:T(8,128)(2,1)}, bf16[256,768]{1,0:T(8,128)(2,1)}, bf16[256,768]{1,0:T(8,128)(2,1)}, bf16[256,768]{1,0:T(8,128)(2,1)}, bf16[2...) conditional(s32[]{:T(128)} %convert_element_type.100, ...), branch_computations={%region_0.0_spmd, %region_1.0_spmd} | conditional | flops 3825205248 | bytes 24000120 | solution.py:727
  19.7 19.8 %encoder_forward.3 = (bf16[256,768]{1,0:T(8,128)(2,1)}, bf16[256,768]{1,0:T(8,128)(2,1)}, bf16[256,768]{1,0:T(8,128)(2,1)}, bf16[256,768]{1,0:T(8,128)(2,1)}, bf...) custom-call(bf16[2,512,768]{2,1,0:T(8,128)(2,1)} %get-tuple-element., ...), custom_call_target="tpu_custom_call" | custom-call | flops 3825205248 | bytes 24000000 | tf_op jit(solution)/shard_map/cond/branch_1_fun/encoder_forward/pallas_call | solution.py:400
  39.5 2.0 collective-permute-start.5
  41.5 20.6 %conditional.8 = (bf16[256,768]{1,0:T(8,128)(2,1)}, bf16[256,768]{1,0:T(8,128)(2,1)}, bf16[256,768]{1,0:T(8,128)(2,1)}, bf16[256,768]{1,0:T(8,128)(2,1)}, bf16[2...) conditional(s32[]{:T(128)} %convert_element_type.100, () %tuple.84, ...), branch_computations={%region_2.0_spmd.clone, %region_3.0_spmd.clone} | conditional | flops 3825205248 | bytes 26359444 | solution.py:727
  41.7 19.6 %encoder_forward.4 = (bf16[256,768]{1,0:T(8,128)(2,1)S(1)}, bf16[256,768]{1,0:T(8,128)(2,1)}, bf16[256,768]{1,0:T(8,128)(2,1)}, bf16[256,768]{1,0:T(8,128)(2,1)}...) custom-call(bf16[2,512,768]{2,1,0:T(8,128)(2,1)} %get-tuple-element., ...), custom_call_target="tpu_custom_call" | custom-call | flops 3825205248 | bytes 24000000 | tf_op jit(solution)/shard_map/cond/branch_1_fun/encoder_forward/pallas_call | solution.py:400
  62.1 2.1 collective-permute-start.6
  64.2 16.9 %conditional.9 = (bf16[256,768]{1,0:T(8,128)(2,1)}, f32[512,768]{1,0:T(8,128)}, f32[8,768]{1,0:T(8,128)S(1)}, f32[2,1,1536]{2,1,0:T(1,128)S(1)}, bf16[256,768]{1...) conditional(s32[]{:T(128)} %convert_element_type.100, ...), branch_computations={%region_4.0_spmd, %region_5.0_spmd} | conditional | flops 9261023232 | bytes 24000120 | solution.py:755
  64.6 16.4 %encoder_targets.2 = bf16[256,768]{1,0:T(8,128)(2,1)} custom-call(bf16[2,512,768]{2,1,0:T(8,128)(2,1)} %get-tuple-element.581.patch_ref, s32[2,512,1]{2,1,0:T(8,128)S(1)} %get-tuple-element.582.order_ref, f32[8,768]{1,0:T(8,128)S(1)} %get-tuple-element.583.vec_ref, f32[2,1,1536]{2,1,0:T(1,128)S(1)} %get-tuple-element.584.bias_ref, ...), custom_call_target="tpu_custom_call" | custom-call | flops 3825205248 | bytes 24000000 | tf_op jit(solution)/shard_map/cond/branch_1_fun/encoder_targets/pallas_call | solution.py:400
  82.4 16.7 %conditional.10 = (bf16[256,768]{1,0:T(8,128)(2,1)}, f32[512,768]{1,0:T(8,128)}, f32[8,768]{1,0:T(8,128)}, f32[2,1,1536]{2,1,0:T(1,128)}, bf16[256,768]{1,0:T(8,...) conditional(s32[]{:T(128)} %convert_element_type.100, ...), branch_computations={%region_6.0_spmd, %region_7.0_spmd} | conditional | flops 9261023232 | bytes 24000120 | solution.py:755
  82.6 16.5 %encoder_targets.3 = bf16[256,768]{1,0:T(8,128)(2,1)} custom-call(bf16[2,512,768]{2,1,0:T(8,128)(2,1)} %get-tuple-element.636.patch_ref, s32[2,512,1]{2,1,0:T(8,128)S(1)} %get-tuple-element.637.order_ref, f32[8,768]{1,0:T(8,128)S(1)} %get-tuple-element.638.vec_ref, f32[2,1,1536]{2,1,0:T(1,128)S(1)} %get-tuple-element.639.bias_ref, ...), custom_call_target="tpu_custom_call" | custom-call | flops 3825205248 | bytes 24000000 | tf_op jit(solution)/shard_map/cond/branch_1_fun/encoder_targets/pallas_call | solution.py:400
  100.4 3.5 collective-permute-done.7
  103.9 24.9 %conditional.11 = (f32[512,768]{1,0:T(8,128)}, f32[8,768]{1,0:T(8,128)S(1)}, f32[2,1,1536]{2,1,0:T(1,128)S(1)}, bf16[256,768]{1,0:T(8,128)(2,1)}, bf16[2,256,153...) conditional(s32[]{:T(128)} %convert_element_type.100, ...), branch_computations={%region_8.0_spmd, %region_9.0_spmd} | conditional | flops 3825205248 | bytes 24004200 | solution.py:777
  104.5 24.3 %encoder_backward.2 = (f32[512,768]{1,0:T(8,128)}, f32[8,768]{1,0:T(8,128)S(1)}, f32[2,1,1536]{2,1,0:T(1,128)S(1)}, bf16[256,768]{1,0:T(8,128)(2,1)}, bf16[2,256...) custom-call(bf16[256,768]{1,0:T(8,128)(2,1)} %get-tuple-element.661., ...), custom_call_target="tpu_custom_call" | custom-call | flops 3825205248 | bytes 24000000 | tf_op jit(solution)/shard_map/cond/branch_1_fun/encoder_backward/pallas_call | solution.py:470
  128.8 17.2 %collective-permute-done.8 = bf16[256,768]{1,0:T(8,128)(2,1)S(1)} collective-permute-done((bf16[256,768]{1,0:T(8,128)(2,1)}, bf16[256,768]{1,0:T(8,128)(2,1)S(1)}, u32[]{:S(2)}, u32[]{:S(2)}) %collective-permute-start.8) | collective-permute-done | bytes 393248 | tf_op jit(solution)/shard_map/ppermute | solution.py:757
  146.8 25.0 %conditional.12 = (f32[512,768]{1,0:T(8,128)}, f32[8,768]{1,0:T(8,128)}, f32[2,1,1536]{2,1,0:T(1,128)}, bf16[256,768]{1,0:T(8,128)(2,1)}, bf16[2,256,1536]{2,1,0...) conditional(s32[]{:T(128)} %convert_element_type.100, ...), branch_computations={%region_10.0_spmd, %region_11.0_spmd} | conditional | flops 3825205248 | bytes 24004200 | solution.py:777
  147.3 24.4 %encoder_backward.3 = (f32[512,768]{1,0:T(8,128)}, f32[8,768]{1,0:T(8,128)}, f32[2,1,1536]{2,1,0:T(1,128)}, bf16[256,768]{1,0:T(8,128)(2,1)}, bf16[2,256,1536]{2...) custom-call(bf16[256,768]{1,0:T(8,128)(2,1)} %get-tuple-element.708., ...), custom_call_target="tpu_custom_call" | custom-call | flops 3825205248 | bytes 24000000 | tf_op jit(solution)/shard_map/cond/branch_1_fun/encoder_backward/pallas_call | solution.py:470
  171.8 25.5 %conditional.13 = (bf16[2,1536,768]{2,1,0:T(8,128)(2,1)}, bf16[2,768,1536]{2,1,0:T(8,128)(2,1)}, bf16[2,384,768]{2,1,0:T(8,128)(2,1)S(1)}, bf16[2,768,384]{2,1,0...) conditional(s32[]{:T(128)} %convert_element_type.100, ...), branch_computations={%region_13.0_spmd, %region_14.0_spmd} | conditional | flops 8455716864 | bytes 57437400 | solution.py:783
  172.0 7.4 %down_grad.3 = bf16[2,1536,768]{2,1,0:T(8,128)(2,1)} custom-call(bf16[2,256,1536]{2,1,0:T(8,128)(2,1)} %get-tuple-element.762.refs_0_, bf16[2,256,1536]{2,1,0:T(8,128)(2,1)} %get-tuple-element.763.refs_1_, bf16[256,768]{1,0:T(8,128)(2,1)} %get-tuple-element.764.refs_2_, bf16[256,768]{1,0:T(8,128)(2,1)} %get-tuple-element.765.refs_3_), custom_call_target="tpu_custom_call" | custom-call | flops 2415919104 | bytes 8000000 | tf_op jit(solution)/shard_map/cond/branch_1_fun/down_grad/pallas_call | solution.py:622
  179.5 2.1 out_grad.3
  181.7 2.2 query_grad.3
  183.9 3.1 key_grad.3
  187.0 3.0 value_grad.3
  190.0 7.3 %up_grad.3 = bf16[2,768,1536]{2,1,0:T(8,128)(2,1)} custom-call(bf16[256,768]{1,0:T(8,128)(2,1)} %get-tuple-element.766.refs_0_, bf16[256,768]{1,0:T(8,128)(2,1)} %get-tuple-element.767.refs_1_, bf16[2,256,1536]{2,1,0:T(8,128)(2,1)} %get-tuple-element.768.refs_2_, bf16[2,256,1536]{2,1,0:T(8,128)(2,1)} %get-tuple-element.769.refs_3_), custom_call_target="tpu_custom_call" | custom-call | flops 2415919104 | bytes 8000000 | tf_op jit(solution)/shard_map/cond/branch_1_fun/up_grad/pallas_call | solution.py:622
  199.4 4.5 collective-permute-done.15
  208.1 4.4 collective-permute-done.13
  217.8 2.0 fusion.4
  223.1 2.0 fusion.5
  231.6 45.2 %reduce-scatter.17.cloned.1.call-done = bf16[192,768]{1,0:T(8,128)(2,1)} async-done(((bf16[1536,768]{1,0:T(8,128)(2,1)}), bf16[192,768]{1,0:T(8,128)(2,1)}) %reduce-scatter.17.cloned.1.call-update) | async-done | bytes 294928 | tf_op jit(solution)/shard_map/reduce_scatter | solution.py:793
  276.9 72.8 %reduce-scatter.15.cloned.1.call-done = bf16[96,1536]{1,0:T(8,128)(2,1)} async-done(((bf16[768,1536]{1,0:T(8,128)(2,1)}), bf16[96,1536]{1,0:T(8,128)(2,1)}) %reduce-scatter.15.cloned.1.call-update) | async-done | bytes 294928 | tf_op jit(solution)/shard_map/reduce_scatter | solution.py:793
  349.7 2.1 maximum_bitcast_fusion.2
  351.8 2.3 maximum_select_fusion
  354.2 59.9 %psum.21 = f32[8,768]{1,0:T(8,128)S(1)} all-reduce(f32[8,768]{1,0:T(8,128)S(1)} %add.45), channel_id=1, replica_groups=mesh['stream'=2,'dp'=8,'head'=2] {'dp','head'}, use_global_device_ids=true, to_apply=%region_12.0 | all-reduce | flops 6144 | bytes 49152 | tf_op jit(solution)/shard_map/psum | solution.py:799
  415.3 3.3 maximum_bitcast_fusion
  418.6 5.5 psum.23
  424.1 18.1 %psum.22 = f32[1,1536]{1,0:T(1,128)} all-reduce(f32[1,1536]{1,0:T(1,128)S(1)} %broadcast_in_dim.74), channel_id=1, replica_groups=mesh['stream'=2,'dp'=8,'head'=2] {'dp'}, use_global_device_ids=true, to_apply=%region_20.0 | all-reduce | flops 1536 | bytes 12288 | tf_op jit(solution)/shard_map/psum | solution.py:798
  442.2 32.0 %all_gather.20 = bf16[768,384]{1,0:T(8,128)(2,1)S(1)} all-gather(bf16[96,384]{1,0:T(8,128)(2,1)} %reduce-scatter.11.cloned.1.call-done), channel_id=1, replica_groups=mesh['stream'=2,'dp'=8,'head'=2] {'dp'}, dimensions={0}, use_global_device_ids=true | all-gather | bytes 663552 | tf_op jit(solution)/shard_map/all_gather | solution.py:794
  474.2 7.2 reduce-scatter.9.cloned.1.call-done
  481.3 32.2 %all_gather.19 = bf16[768,384]{1,0:T(8,128)(2,1)S(1)} all-gather(bf16[96,384]{1,0:T(8,128)(2,1)} %reduce-scatter.9.cloned.1.call-done), channel_id=1, replica_groups=mesh['stream'=2,'dp'=8,'head'=2] {'dp'}, dimensions={0}, use_global_device_ids=true | all-gather | bytes 663552 | tf_op jit(solution)/shard_map/all_gather | solution.py:794
  513.5 33.5 %reduce-scatter.7.cloned.1.call-done = bf16[96,384]{1,0:T(8,128)(2,1)} async-done(((bf16[768,384]{1,0:T(8,128)(2,1)}), bf16[96,384]{1,0:T(8,128)(2,1)}) %reduce-scatter.7.cloned.1.call-update) | async-done | bytes 73744 | tf_op jit(solution)/shard_map/reduce_scatter | solution.py:793
  547.0 32.2 %all_gather.18 = bf16[768,384]{1,0:T(8,128)(2,1)S(1)} all-gather(bf16[96,384]{1,0:T(8,128)(2,1)} %reduce-scatter.7.cloned.1.call-done), channel_id=1, replica_groups=mesh['stream'=2,'dp'=8,'head'=2] {'dp'}, dimensions={0}, use_global_device_ids=true | all-gather | bytes 663552 | tf_op jit(solution)/shard_map/all_gather | solution.py:794
  579.2 2.1 fusion.2
  581.2 30.7 %reduce-scatter.13.cloned.1.call-done = bf16[48,768]{1,0:T(8,128)(2,1)} async-done(((bf16[384,768]{1,0:T(8,128)(2,1)}), bf16[48,768]{1,0:T(8,128)(2,1)}) %reduce-scatter.13.cloned.1.call-update) | async-done | bytes 73744 | tf_op jit(solution)/shard_map/reduce_scatter | solution.py:793
  612.0 32.8 %all_gather.21 = bf16[384,768]{1,0:T(8,128)(2,1)S(1)} all-gather(bf16[48,768]{1,0:T(8,128)(2,1)} %reduce-scatter.13.cloned.1.call-done), channel_id=1, replica_groups=mesh['stream'=2,'dp'=8,'head'=2] {'dp'}, dimensions={0}, use_global_device_ids=true | all-gather | bytes 663552 | tf_op jit(solution)/shard_map/all_gather | solution.py:794
  645.9 20.9 %all-gather.5.cloned.1.call-done = bf16[1536,768]{1,0:T(8,128)(2,1)} async-done(((bf16[192,768]{1,0:T(8,128)(2,1)}), bf16[1536,768]{1,0:T(8,128)(2,1)}) %all-gather.5.cloned.1.call-update) | async-done | bytes 2359312 | tf_op jit(solution)/shard_map/all_gather | solution.py:794
  666.8 4.2 bitcast_convert_fusion
  671.0 48.4 %all-gather.3.cloned.1.call-done = bf16[768,1536]{1,0:T(8,128)(2,1)} async-done(((bf16[96,1536]{1,0:T(8,128)(2,1)}), bf16[768,1536]{1,0:T(8,128)(2,1)}) %all-gather.3.cloned.1.call-update) | async-done | bytes 2359312 | tf_op jit(solution)/shard_map/all_gather | solution.py:794
  719.4 4.5 bitcast_convert_fusion.1
  (112 shorter events, 33.7 us)
Async XLA Ops:
  7.2 269.6 %reduce-scatter.17.cloned.1.call-start = ((), (), s32[]{:S(2)}) async-start(), calls=%async_computation.12 | async-start | bytes 2654208 | tf_op jit(solution)/shard_map/reduce_scatter | solution.py:793
  7.2 12.4 %collective-permute-start.3 = (bf16[768,1536]{1,0:T(8,128)(2,1)}, bf16[768,1536]{1,0:T(8,128)(2,1)S(1)}, u32[]{:S(2)}, u32[]{:S(2)}) collective-permute-start(bf16[768,1536]{1,0:T(8,128)(2,1)} %bitcast.76), channel_id=1, source_target_pairs={{0,1},{1,0},{2,3},{3,2},{4,5},{5,4},{6,7},{7,6},{8,9},{9,8},{10,11... | collective-permute-start | bytes 7077896 | tf_op jit(solution)/shard_map/ppermute | solution.py:684
  7.8 11.9 %collective-permute-start.4 = (bf16[1536,768]{1,0:T(8,128)(2,1)}, bf16[1536,768]{1,0:T(8,128)(2,1)}, u32[]{:S(2)}, u32[]{:S(2)}) collective-permute-start(bf16[1536,768]{1,0:T(8,128)(2,1)} %bitcast.85), channel_id=1, source_target_pairs={{0,1},{1,0},{2,3},{3,2},{4,5},{5,4},{6,7},{7,6},{8,9},{9,8},{10,11... | collective-permute-start | bytes 7077896 | tf_op jit(solution)/shard_map/ppermute | solution.py:684
  7.9 11.8 %collective-permute-start.1 = (bf16[3,768,384]{2,1,0:T(8,128)(2,1)}, bf16[3,768,384]{2,1,0:T(8,128)(2,1)}, u32[]{:S(2)}, u32[]{:S(2)}) collective-permute-start(bf16[3,768,384]{2,1,0:T(8,128)(2,1)} %bitcast.94), channel_id=1, source_target_pairs={{0,1},{1,0},{2,3},{3,2},{4,5},{5,4},{6,7},{7,6},{8,9},{9,8},{10,11... | collective-permute-start | bytes 5308424 | tf_op jit(solution)/shard_map/ppermute | solution.py:684
  8.3 11.3 %collective-permute-start.2 = (bf16[384,768]{1,0:T(8,128)(2,1)}, bf16[384,768]{1,0:T(8,128)(2,1)S(1)}, u32[]{:S(2)}, u32[]{:S(2)}) collective-permute-start(bf16[384,768]{1,0:T(8,128)(2,1)} %bitcast.103), channel_id=1, source_target_pairs={{0,1},{1,0},{2,3},{3,2},{4,5},{5,4},{6,7},{7,6},{8,9},{9,8},{10,11... | collective-permute-start | bytes 1769480 | tf_op jit(solution)/shard_map/ppermute | solution.py:684
  9.1 9.8 %collective-permute-start = (bf16[1536]{0:T(1024)(128)(2,1)S(1)}, bf16[1536]{0:T(1024)(128)(2,1)S(1)}, u32[]{:S(2)}, u32[]{:S(2)}) collective-permute-start(bf16[1536]{0:T(1024)(128)(2,1)S(1)} %reduce), channel_id=1, source_target_pairs={{0,1},{1,0},{2,3},{3,2},{4,5},{5,4},{6,7},{7,6},{8,9},{9,8},{10,11... | collective-permute-start | bytes 9224 | tf_op jit(solution)/shard_map/ppermute | solution.py:684
  39.5 24.7 %collective-permute-start.5 = (bf16[256,768]{1,0:T(8,128)(2,1)}, bf16[256,768]{1,0:T(8,128)(2,1)}, u32[]{:S(2)}, u32[]{:S(2)}) collective-permute-start(bf16[256,768]{1,0:T(8,128)(2,1)} %get-tuple-element.886), channel_id=1, source_target_pairs={{0,16},{1,17},{2,18},{3,19},{4,20},{5,21},{6,22},{7,23},{8,24},{9,... | collective-permute-start | bytes 1179656 | tf_op jit(solution)/shard_map/ppermute | solution.py:733
  41.5 22.6 %copy-start.21 = (f32[768]{0:T(1024)S(1)}, f32[768]{0:T(1024)}, u32[]{:S(2)}) copy-start(f32[768]{0:T(1024)} %param.39) | copy-start | bytes 9220
  61.3 0.8 copy-start.4
  62.1 2.1 copy-start.5
  62.1 20.3 %collective-permute-start.6 = (bf16[256,768]{1,0:T(8,128)(2,1)}, bf16[256,768]{1,0:T(8,128)(2,1)}, u32[]{:S(2)}, u32[]{:S(2)}) collective-permute-start(bf16[256,768]{1,0:T(8,128)(2,1)} %get-tuple-element.887), channel_id=1, source_target_pairs={{0,16},{1,17},{2,18},{3,19},{4,20},{5,21},{6,22},{7,23},{8,24},{9,... | collective-permute-start | bytes 1179656 | tf_op jit(solution)/shard_map/ppermute | solution.py:733
  81.1 22.8 %collective-permute-start.7 = (bf16[256,768]{1,0:T(8,128)(2,1)}, bf16[256,768]{1,0:T(8,128)(2,1)}, u32[]{:S(2)}, u32[]{:S(2)}) collective-permute-start(bf16[256,768]{1,0:T(8,128)(2,1)} %get-tuple-element.894), channel_id=1, source_target_pairs={{16,0},{17,1},{18,2},{19,3},{20,4},{21,5},{22,6},{23,7},{24,8},{25... | collective-permute-start | bytes 1179656 | tf_op jit(solution)/shard_map/ppermute | solution.py:757
  82.4 18.0 %copy-start.18 = (s32[2,512]{1,0:T(2,128)S(1)}, s32[2,512]{1,0:T(2,128)}, u32[]{:S(2)}) copy-start(s32[2,512]{1,0:T(2,128)} %param.28) | copy-start | bytes 12292
  99.1 46.9 %collective-permute-start.8 = (bf16[256,768]{1,0:T(8,128)(2,1)}, bf16[256,768]{1,0:T(8,128)(2,1)S(1)}, u32[]{:S(2)}, u32[]{:S(2)}) collective-permute-start(bf16[256,768]{1,0:T(8,128)(2,1)} %get-tuple-element.912), channel_id=1, source_target_pairs={{16,0},{17,1},{18,2},{19,3},{20,4},{21,5},{22,6},{23,7},{24,8},{25... | collective-permute-start | bytes 1179656 | tf_op jit(solution)/shard_map/ppermute | solution.py:757
  146.0 0.7 copy-start.17
  146.8 25.0 %copy-start = (bf16[256,768]{1,0:T(8,128)(2,1)S(1)}, bf16[256,768]{1,0:T(8,128)(2,1)}, u32[]{:S(2)}) copy-start(bf16[256,768]{1,0:T(8,128)(2,1)} %get-tuple-element.961) | copy-start | bytes 1179652
  172.0 7.4 %copy-start.8 = (bf16[256,768]{1,0:T(8,128)(2,1)S(1)}, bf16[256,768]{1,0:T(8,128)(2,1)}, u32[]{:S(2)}) copy-start(bf16[256,768]{1,0:T(8,128)(2,1)} %get-tuple-element.770.refs_0_) | copy-start | bytes 1179652 | tf_op jit(solution)/shard_map/cond
  172.0 7.4 %copy-start.9 = (bf16[256,768]{1,0:T(8,128)(2,1)S(1)}, bf16[256,768]{1,0:T(8,128)(2,1)}, u32[]{:S(2)}) copy-start(bf16[256,768]{1,0:T(8,128)(2,1)} %get-tuple-element.771.refs_1_) | copy-start | bytes 1179652 | tf_op jit(solution)/shard_map/cond
  172.0 7.4 %copy-start.14 = (bf16[256,768]{1,0:T(8,128)(2,1)S(1)}, bf16[256,768]{1,0:T(8,128)(2,1)}, u32[]{:S(2)}) copy-start(bf16[256,768]{1,0:T(8,128)(2,1)} %get-tuple-element.772.refs_2_) | copy-start | bytes 1179652 | tf_op jit(solution)/shard_map/cond
  179.5 2.2 copy-start.1
  179.5 2.2 copy-start.15
  183.9 3.1 copy-start.16
  197.3 6.6 copy-start.2
  199.3 4.6 collective-permute-start.15
  205.9 143.8 %reduce-scatter.15.cloned.1.call-start = ((), (), s32[]{:S(2)}) async-start(), calls=%async_computation.10 | async-start | bytes 2654208 | tf_op jit(solution)/shard_map/reduce_scatter | solution.py:793
  206.0 6.6 copy-start.3
  207.9 4.6 collective-permute-start.13
  214.6 227.6 %reduce-scatter.11.cloned.1.call-start = ((), (), s32[]{:S(2)}) async-start(), calls=%async_computation.8 | async-start | bytes 663552 | tf_op jit(solution)/shard_map/reduce_scatter | solution.py:793
  215.8 2.1 collective-permute-start.11
  219.9 261.4 %reduce-scatter.9.cloned.1.call-start = ((), (), s32[]{:S(2)}) async-start(), calls=%async_computation.7 | async-start | bytes 663552 | tf_op jit(solution)/shard_map/reduce_scatter | solution.py:793
  221.1 2.1 collective-permute-start.10
  225.2 321.8 %reduce-scatter.7.cloned.1.call-start = ((), (), s32[]{:S(2)}) async-start(), calls=%async_computation.6 | async-start | bytes 663552 | tf_op jit(solution)/shard_map/reduce_scatter | solution.py:793
  225.3 2.1 collective-permute-start.9
  228.4 383.6 %reduce-scatter.13.cloned.1.call-start = ((), (), s32[]{:S(2)}) async-start(), calls=%async_computation.9 | async-start | bytes 663552 | tf_op jit(solution)/shard_map/reduce_scatter | solution.py:793
  228.5 2.1 collective-permute-start.12
  231.5 120.3 %copy-start.6 = (bf16[1,256,768]{2,1,0:T(8,128)(2,1)S(1)}, bf16[1,256,768]{2,1,0:T(8,128)(2,1)}, u32[]{:S(2)}) copy-start(bf16[1,256,768]{2,1,0:T(8,128)(2,1)} %copy-done.5) | copy-start | bytes 1179652
  231.5 120.3 %copy-start.10 = (bf16[256,768]{1,0:T(8,128)(2,1)S(1)}, bf16[256,768]{1,0:T(8,128)(2,1)}, u32[]{:S(2)}) copy-start(bf16[256,768]{1,0:T(8,128)(2,1)} %get-tuple-element.886) | copy-start | bytes 1179652
  231.5 435.3 %all-gather.5.cloned.1.call-start = ((), (), s32[]{:S(2)}) async-start(), calls=%async_computation.13 | async-start | bytes 2654208 | tf_op jit(solution)/shard_map/all_gather | solution.py:794
  276.8 442.5 %all-gather.3.cloned.1.call-start = ((), (), s32[]{:S(2)}) async-start(), calls=%async_computation.11 | async-start | bytes 2654208 | tf_op jit(solution)/shard_map/all_gather | solution.py:794
  351.8 2.3 copy-start.20
  351.8 2.4 copy-start.19
  351.8 63.5 %copy-start.7 = (f32[512,768]{1,0:T(8,128)S(1)}, f32[512,768]{1,0:T(8,128)}, u32[]{:S(2)}) copy-start(f32[512,768]{1,0:T(8,128)} %get-tuple-element.908) | copy-start | bytes 4718596
  354.1 70.0 %collective-permute-start.14 = (f32[1536]{0:T(1024)S(1)}, f32[1536]{0:T(1024)S(1)}, u32[]{:S(2)}, u32[]{:S(2)}) collective-permute-start(f32[1536]{0:T(1024)S(1)} %get-tuple-element.1122), channel_id=1, source_target_pairs={{0,1},{1,0},{2,3},{3,2},{4,5},{5,4},{6,7},{7,6},{8,9},{9,8},{10,11... | collective-permute-start | bytes 18440 | tf_op jit(solution)/shard_map/ppermute | solution.py:684
Sparse Core Ops, SparseCore 0:
  206.0 70.7 reduce-scatter.16
  280.8 68.8 reduce-scatter.14
  353.6 61.9 reduce-scatter.10
  419.3 62.0 reduce-scatter.8
  485.0 61.9 reduce-scatter.6
  550.1 61.7 reduce-scatter.12
  614.2 52.5 all-gather.4
  669.0 50.3 all-gather.2
